TPU v7x, 32 devices: a whole 2x2x4 slice. The times are simulated.
32 devices in a mesh: seq: 8 (over y, x, core), cb: 4 (over z).
Axes of the slice: x: 2, y: 2, z: 4, core: 2. Of those that a mesh axis runs over, the one named last changes fastest.
Arguments:
- hidden: bfloat16 [2, 1024, 4096], P(None, 'seq'), may hold values from -6 to 6
- temporal_gain: float32 [4096], replicated, may hold values from 0.5 to 2
- temporal_qkv: bfloat16 [3, 4096, 2048], P(None, None, 'cb'), may hold values from -10 to 10
- temporal_out: bfloat16 [2048, 4096], P('cb'), may hold values from -0.125 to 0.125
- codebook_ids: int32 [2, 1024, 4], P(None, 'seq', 'cb'), may hold values from 0 to 2047
- embedding: bfloat16 [4, 2048, 1024], P('cb'), may hold values from -6 to 6
- input_weight: bfloat16 [4, 4096, 1024], P('cb', 'seq'), may hold values from -0.09375 to 0.09375
- depth_gain: float32 [4, 1024], P('cb'), may hold values from 0.5 to 2
- depth_qkv: bfloat16 [4, 3, 1024, 1024], P('cb'), may hold values from -10 to 10
- depth_out: bfloat16 [4, 1024, 1024], P('cb'), may hold values from -0.1875 to 0.1875
Outputs:
- temporal: bfloat16 [2, 1024, 4096], P(None, 'seq')
- depth: bfloat16 [2, 1024, 4, 1024], P(None, 'seq', 'cb')
All inputs are finite; a program needn't handle non-finite values.
Results may differ from a plain program's by a relative error of at most 0.017.
Values may be sent and summed in bfloat16 or wider, within the bound.
No kernel may reach another device: no remote copies, remote signals or barrier semaphores. Data moves between devices by JAX's collectives and lax.ppermute only.
A program may use at most 128 MiB of HBM per device.

v0:
```python
import functools

import jax
import jax.numpy as jnp
from jax import lax
from jax.experimental import pallas as pl
from jax.experimental.pallas import tpu as pltpu
from jax.sharding import PartitionSpec as P


HD = 128
DHD = 64
EPS = 1e-05
NEG = -1e30
F32 = jnp.float32
BF16 = jnp.bfloat16
CHUNKS = 2
VMEM_LIMIT = 60 * 1024 * 1024


VM = pl.BlockSpec(memory_space=pltpu.VMEM)
SM = pl.BlockSpec(memory_space=pltpu.SMEM)
ANY = pl.BlockSpec(memory_space=pl.ANY)
PARAMS = pltpu.CompilerParams(vmem_limit_bytes=VMEM_LIMIT)


def cost(flops, moved):
    return pl.CostEstimate(flops=flops, bytes_accessed=moved, transcendentals=0)


def dot(a, b):
    return jnp.dot(a, b, preferred_element_type=F32)


def flip(x, axis, bit):
    return lax.ppermute(x, axis, [(i, i ^ bit) for i in range(lax.axis_size(axis))])


def shift(x, axis, by):
    size = lax.axis_size(axis)
    return lax.ppermute(x, axis, [(i, (i + by) % size) for i in range(size)])


def ici_bits(size):
    return [1 << place for place in range(1, size.bit_length() - 1)]


def spread(piece, axis, order):
    held = {0: piece}
    for bit in order:
        held.update({at ^ bit: flip(v, axis, bit) for at, v in list(held.items())})
    held.update({at ^ 1: flip(v, axis, 1) for at, v in list(held.items())})
    return held


def spread_halves(first, second, axis):
    size = lax.axis_size(axis)
    a = spread(first, axis, ici_bits(size))
    b = spread(second, axis, ici_bits(size)[::-1])
    return [half for at in range(size) for half in (a[at], b[at])]


def project_body(hidden_ref, gain_ref, weight_ref, out_ref, normed_ref):
    seqs, heads, frames, _ = out_ref.shape
    rows = normed_ref.shape[0]
    step = min(64, rows)

    @pl.when(pl.program_id(0) == 0)
    def _():
        def one(at, carry):
            span = pl.ds(pl.multiple_of(at * step, step), step)
            values = hidden_ref[span, :].astype(F32)
            mean_sq = jnp.mean(values * values, axis=-1, keepdims=True)
            normed_ref[span, :] = (values * lax.rsqrt(mean_sq + EPS) * gain_ref[...]).astype(BF16)
            return carry

        lax.fori_loop(0, rows // step, one, 0)

    result = dot(normed_ref[...], weight_ref[0]).astype(BF16)
    for s in range(seqs):
        for h in range(heads):
            out_ref[s, h] = result[s * frames : (s + 1) * frames, h * HD : (h + 1) * HD]


def project(hidden, gain, weight):
    seqs, frames, width = hidden.shape
    cols = weight.shape[2]
    heads = cols // HD
    per = min(2, heads)
    parts = heads // per
    rows = seqs * frames
    return pl.pallas_call(
        project_body,
        grid=(3 * parts,),
        in_specs=[
            pl.BlockSpec((rows, width), lambda i: (0, 0)),
            pl.BlockSpec((1, width), lambda i: (0, 0)),
            pl.BlockSpec((1, width, per * HD), lambda i: (i // parts, 0, i % parts)),
        ],
        out_specs=pl.BlockSpec((seqs, per, frames, HD), lambda i: (0, i % parts, 0, i // parts)),
        out_shape=jax.ShapeDtypeStruct((seqs, heads, frames, 3 * HD), BF16),
        scratch_shapes=[pltpu.VMEM((rows, width), BF16)],
        compiler_params=PARAMS,
        cost_estimate=cost(6 * rows * width * cols, 6 * width * cols + 2 * rows * width),
    )(hidden.reshape(rows, width), gain.reshape(1, width), weight)


def attend_body(packed_ref, out_ref):
    length = packed_ref.shape[0]
    block = min(256, length)
    scale = 1.0 / (HD**0.5)
    for start in range(0, length, block):
        stop = start + block
        scores = (
            lax.dot_general(
                packed_ref[start:stop, :HD],
                packed_ref[:stop, HD : 2 * HD],
                (((1,), (1,)), ((), ())),
                preferred_element_type=F32,
            )
            * scale
        )
        rows = lax.broadcasted_iota(jnp.int32, scores.shape, 0) + start
        cols = lax.broadcasted_iota(jnp.int32, scores.shape, 1)
        scores = jnp.where(cols <= rows, scores, NEG)
        weights = jnp.exp(scores - jnp.max(scores, axis=-1, keepdims=True))
        totals = jnp.sum(weights, axis=-1, keepdims=True)
        mixed = dot(weights.astype(BF16), packed_ref[:stop, 2 * HD :])
        out_ref[start:stop, :] = (mixed / totals).astype(BF16)


def attend_pair(packed):
    length = packed.shape[0]
    return pl.pallas_call(
        attend_body,
        in_specs=[VM],
        out_specs=VM,
        out_shape=jax.ShapeDtypeStruct((length, HD), BF16),
        compiler_params=PARAMS,
        cost_estimate=cost(3 * length * length * HD, 8 * length * HD),
    )(packed)


def temporal_attention(packed):
    seqs, heads, frames, _ = packed.shape
    pairs = seqs * heads
    size = lax.axis_size("seq")
    if pairs == size:
        whole = lax.all_to_all(packed.reshape(pairs, frames, 3 * HD), "seq", split_axis=0, concat_axis=0, tiled=True)
        mixed = attend_pair(whole.reshape(size * frames, 3 * HD))
        return lax.all_to_all(
            mixed.reshape(size, frames, HD), "seq", split_axis=0, concat_axis=0, tiled=True
        )
    queries = packed[..., :HD]
    both = lax.all_gather(packed[..., HD:], "seq", axis=2, tiled=True)
    keys, values = both[..., :HD], both[..., HD:]
    scores = jnp.einsum("shqd,shkd->shqk", queries, keys, preferred_element_type=F32) / (HD**0.5)
    at = lax.axis_index("seq") * frames + jnp.arange(frames, dtype=jnp.int32)
    allowed = jnp.arange(size * frames, dtype=jnp.int32)[None, :] <= at[:, None]
    scores = jnp.where(allowed, scores, NEG)
    weights = jnp.exp(scores - jnp.max(scores, axis=-1, keepdims=True))
    totals = jnp.sum(weights, axis=-1, keepdims=True)
    mixed = jnp.einsum(
        "shqk,shkd->shqd", weights.astype(BF16), values, preferred_element_type=F32
    )
    return (mixed / totals).astype(BF16).reshape(pairs, frames, HD)


def output_body(place_ref, hidden_ref, *refs):
    books = place_ref.shape[0] - 2
    del books
    mixed_refs, (own_ref,), pieces, (out_ref, cat_ref, weight_ref, sems) = refs
    size, groups, _, half, block = weight_ref.shape
    seqs_heads, frames, _ = mixed_refs[0].shape
    cols = 2 * half
    heads = cols // HD
    me = place_ref[0]

    def copies(at):
        column = pl.multiple_of((me ^ at) * block, block)
        found = []
        for side in range(2):
            found.append(
                pltpu.make_async_copy(
                    own_ref.at[side * half : (side + 1) * half, pl.ds(column, block)],
                    weight_ref.at[at, 0, side],
                    sems.at[at, side],
                )
            )
            found.append(
                pltpu.make_async_copy(
                    pieces[2 * at + side], weight_ref.at[at, 1:, side], sems.at[at, 2 + side]
                )
            )
        return found

    for at in range(size):
        for copy in copies(at):
            copy.start()
    for group in range(groups):
        for pair in range(seqs_heads):
            s, h = pair // heads, pair % heads
            cat_ref[s * frames : (s + 1) * frames, group * cols + h * HD : group * cols + (h + 1) * HD] = (
                mixed_refs[group][pair]
            )
    for at in range(size):
        for copy in copies(at):
            copy.wait()
        span = pl.ds(pl.multiple_of((me ^ at) * block, block), block)
        summed = dot(cat_ref[...], weight_ref[at].reshape(groups * cols, block))
        out_ref[:, span] = (hidden_ref[:, span].astype(F32) + summed).astype(BF16)


def temporal_output(place, hidden, mixed, own, pieces):
    rows, width = hidden.shape
    cols = own.shape[0]
    groups = len(mixed)
    size = len(pieces) // 2
    block = width // size

    def body(place_ref, hidden_ref, *refs):
        refs = list(refs)
        output_body(
            place_ref,
            hidden_ref,
            refs[:groups],
            refs[groups : groups + 1],
            refs[groups + 1 : groups + 1 + 2 * size],
            refs[groups + 1 + 2 * size :],
        )

    return pl.pallas_call(
        body,
        in_specs=[SM, VM] + [VM] * groups + [ANY] * (1 + 2 * size),
        out_specs=VM,
        out_shape=jax.ShapeDtypeStruct((rows, width), BF16),
        scratch_shapes=[
            pltpu.VMEM((rows, groups * cols), BF16),
            pltpu.VMEM((size, groups, 2, cols // 2, block), BF16),
            pltpu.SemaphoreType.DMA((size, 4)),
        ],
        compiler_params=PARAMS,
        cost_estimate=cost(2 * rows * groups * cols * width, 2 * groups * cols * width),
    )(place, hidden, *mixed, own, *pieces)


def put_qkv(normed, weights, out_refs, full_ref, book):
    books = len(out_refs)
    block, wide = out_refs[0].shape
    cols = wide // 3
    for which in range(3):
        full_ref[:, which * cols : (which + 1) * cols] = dot(normed, weights[which])
    for at in range(books):
        row = pl.multiple_of(lax.rem(book + at, books) * block, block)
        out_refs[at][...] = full_ref[pl.ds(row, block), :].astype(BF16)


def stream_kernel(place, temporal, pieces, entry, gain, weights, books, chunks):
    rows, width = temporal.shape
    size = len(pieces) // 2
    half, deep = pieces[0].shape
    block = rows // books
    cols = deep // chunks
    chips = size // 2

    def body(place_ref, temporal_ref, entry_ref, gain_ref, qkv_ref, *refs):
        piece_refs = refs[: 2 * size]
        stream_ref, normed_ref = refs[2 * size : 2 * size + 2]
        out_refs = refs[2 * size + 2 : 2 * size + 2 + books]
        weight_ref, qkv_buf, acc_ref, full_ref, sems, qkv_sem = refs[2 * size + 2 + books :]
        me = place_ref[0]
        book = place_ref[1]

        def copies(chip):
            found = []
            for core in range(2):
                at = 2 * chip + core
                where = (me ^ at) & 1
                for side in range(2):
                    found.append(
                        pltpu.make_async_copy(
                            piece_refs[2 * at + side],
                            weight_ref.at[chip, where, side],
                            sems.at[chip, 2 * core + side],
                        )
                    )
            return found

        fetch = pltpu.make_async_copy(qkv_ref.at[:, :, 0:cols], qkv_buf, qkv_sem.at[0])
        for chip in range(chips):
            for copy in copies(chip):
                copy.start()
        fetch.start()
        for chip in range(chips):
            for copy in copies(chip):
                copy.wait()
            start = pl.multiple_of(lax.shift_right_logical(me ^ (2 * chip), 1) * 4 * half, 4 * half)
            term = dot(temporal_ref[:, pl.ds(start, 4 * half)], weight_ref[chip].reshape(4 * half, deep))
            if chip == 0:
                acc_ref[...] = term
            else:
                acc_ref[...] += term
        stream = (acc_ref[...] + entry_ref[...].astype(F32)).astype(BF16)
        stream_ref[...] = stream
        values = stream.astype(F32)
        mean_sq = jnp.mean(values * values, axis=-1, keepdims=True)
        normed_ref[...] = (values * lax.rsqrt(mean_sq + EPS) * gain_ref[...]).astype(BF16)
        fetch.wait()
        put_qkv(normed_ref[...], qkv_buf, out_refs, full_ref, book)

    return pl.pallas_call(
        body,
        in_specs=[SM, VM, VM, VM, ANY] + [ANY] * (2 * size),
        out_specs=[VM] * (2 + books),
        out_shape=[jax.ShapeDtypeStruct((rows, deep), BF16)] * 2
        + [jax.ShapeDtypeStruct((block, 3 * cols), BF16)] * books,
        scratch_shapes=[
            pltpu.VMEM((chips, 2, 2, half, deep), BF16),
            pltpu.VMEM((3, deep, cols), BF16),
            pltpu.VMEM((rows, deep), F32),
            pltpu.VMEM((rows, 3 * cols), F32),
            pltpu.SemaphoreType.DMA((chips, 4)),
            pltpu.SemaphoreType.DMA((1,)),
        ],
        compiler_params=PARAMS,
        cost_estimate=cost(2 * rows * width * deep + 6 * rows * deep * cols, 2 * width * deep + 6 * deep * cols),
    )(place, temporal, entry, gain, weights, *pieces)


def qkv_kernel(place, normed, weights, books, part, chunks):
    rows, deep = normed.shape
    cols = deep // chunks
    block = rows // books

    def body(place_ref, normed_ref, qkv_ref, *refs):
        put_qkv(normed_ref[...], qkv_ref, refs[:books], refs[books], place_ref[1])

    return pl.pallas_call(
        body,
        grid=(1,),
        in_specs=[
            SM,
            pl.BlockSpec((rows, deep), lambda i: (0, 0)),
            pl.BlockSpec((3, deep, cols), lambda i: (0, 0, part)),
        ],
        out_specs=[pl.BlockSpec((block, 3 * cols), lambda i: (0, 0))] * books,
        out_shape=[jax.ShapeDtypeStruct((block, 3 * cols), BF16)] * books,
        scratch_shapes=[pltpu.VMEM((rows, 3 * cols), F32)],
        compiler_params=PARAMS,
        cost_estimate=cost(6 * rows * deep * cols, 6 * deep * cols),
    )(place, normed, weights)


def two(values):
    high = values.astype(BF16)
    return high, (values - high.astype(F32)).astype(BF16)


def depth_attention(place, arrived):
    books = len(arrived)
    rows, wide = arrived[0].shape
    cols = wide // 3
    scale = 1.0 / (DHD**0.5)

    def body(place_ref, *refs):
        arrived_refs = refs[:books]
        out_refs = refs[books : 2 * books]
        all_ref, result_ref = refs[2 * books :]
        book = place_ref[1]
        for at in range(books):
            all_ref[lax.rem(book + books - at, books)] = arrived_refs[at][...]
        lane = lax.broadcasted_iota(jnp.int32, (cols, 128), 0) // DHD
        head = lax.broadcasted_iota(jnp.int32, (cols, 128), 1)
        gather = (lane == head).astype(BF16)
        lane_t = lax.broadcasted_iota(jnp.int32, (128, cols), 1) // DHD
        head_t = lax.broadcasted_iota(jnp.int32, (128, cols), 0)
        scatter = (lane_t == head_t).astype(BF16)
        for c in range(books):
            query = all_ref[c, :, :cols].astype(F32)
            scores = []
            for j in range(c + 1):
                high, low = two(query * all_ref[j, :, cols : 2 * cols].astype(F32))
                scores.append((dot(high, gather) + dot(low, gather)) * scale)
            highest = functools.reduce(jnp.maximum, scores)
            weights = [jnp.exp(score - highest) for score in scores]
            inverse = 1.0 / functools.reduce(jnp.add, weights)
            mixed = jnp.zeros((rows, cols), F32)
            for j in range(c + 1):
                mixed += dot(weights[j].astype(BF16), scatter) * all_ref[j, :, 2 * cols :].astype(F32)
            high, low = two(inverse)
            mixed = mixed * (dot(high, scatter) + dot(low, scatter))
            result_ref[c] = mixed.astype(BF16)
        for at in range(books):
            out_refs[at][...] = result_ref[lax.rem(book + at, books)]

    return pl.pallas_call(
        body,
        in_specs=[SM] + [VM] * books,
        out_specs=[VM] * books,
        out_shape=[jax.ShapeDtypeStruct((rows, cols), BF16)] * books,
        scratch_shapes=[pltpu.VMEM((books, rows, wide), BF16), pltpu.VMEM((books, rows, cols), BF16)],
        compiler_params=PARAMS,
        cost_estimate=cost(4 * books * books * rows * cols * 128, 8 * books * rows * cols),
    )(place, *arrived)


def depth_output(place, stream, returned, weight):
    rows, deep = stream.shape
    chunks = len(returned)
    books = len(returned[0])
    block = rows // books
    cols = deep // chunks
    flat = [value for part in returned for value in part]

    def body(place_ref, stream_ref, weight_ref, *refs):
        parts = refs[: chunks * books]
        out_ref, cat_ref = refs[chunks * books :]
        book = place_ref[1]
        for k in range(chunks):
            for at in range(books):
                row = pl.multiple_of(lax.rem(book + books - at, books) * block, block)
                cat_ref[pl.ds(row, block), k * cols : (k + 1) * cols] = parts[k * books + at][...]
        result = dot(cat_ref[...], weight_ref[...]) + stream_ref[...].astype(F32)
        out_ref[...] = result.astype(BF16)

    return pl.pallas_call(
        body,
        in_specs=[SM] + [VM] * (2 + chunks * books),
        out_specs=VM,
        out_shape=jax.ShapeDtypeStruct((rows, deep), BF16),
        scratch_shapes=[pltpu.VMEM((rows, deep), BF16)],
        compiler_params=PARAMS,
        cost_estimate=cost(2 * rows * deep * deep, 2 * deep * deep),
    )(place, stream, weight, *flat)


def shards(
    hidden,
    temporal_gain,
    temporal_qkv,
    temporal_out,
    codebook_ids,
    embedding,
    input_weight,
    depth_gain,
    depth_qkv,
    depth_out,
):
    seqs, frames, width = hidden.shape
    rows = seqs * frames
    deep = depth_gain.shape[1]
    cols = temporal_out.shape[0]
    size = lax.axis_size("seq")
    books = lax.axis_size("cb")
    place = jnp.stack([lax.axis_index("seq"), lax.axis_index("cb")]).astype(jnp.int32)

    block = width // size
    ring = [lax.dynamic_slice_in_dim(temporal_out, lax.axis_index("seq") * block, block, 1)]
    for _ in range(1, books):
        ring.append(shift(ring[-1], "cb", 1))
    half = input_weight.shape[1] // 2
    in_pieces = spread_halves(input_weight[0, :half], input_weight[0, half:], "seq")
    half = cols // 2
    first = jnp.stack([piece[:half] for piece in ring[1:]])
    second = jnp.stack([piece[half:] for piece in ring[1:]])
    out_pieces = spread_halves(first, second, "seq")

    entry = jnp.take(embedding[0], codebook_ids.reshape(rows), axis=0)

    packed = project(hidden, temporal_gain, temporal_qkv)
    own_mixed = temporal_attention(packed)
    mixed = [own_mixed] + [shift(own_mixed, "cb", by) for by in range(1, books)]
    temporal = temporal_output(
        place, hidden.reshape(rows, width), mixed, temporal_out, out_pieces
    )
    stream, normed, *sent = stream_kernel(place, temporal, in_pieces, entry, depth_gain, depth_qkv[0], books, CHUNKS)
    arrived, returned = [], []
    for part in range(CHUNKS):
        if part > 0:
            sent = qkv_kernel(place, normed, depth_qkv[0], books, part, CHUNKS)
        arrived.append([sent[0]] + [shift(sent[by], "cb", by) for by in range(1, books)])
    for part in range(CHUNKS):
        result = depth_attention(place, arrived[part])
        returned.append([result[0]] + [shift(result[by], "cb", by) for by in range(1, books)])
    depth = depth_output(place, stream, returned, depth_out[0])
    return (temporal.reshape(seqs, frames, width), depth.reshape(seqs, frames, 1, deep))


def solution(mesh):
    placed = (
        P(None, "seq", None),
        P(),
        P(None, None, "cb"),
        P("cb", None),
        P(None, "seq", "cb"),
        P("cb", None, None),
        P("cb", "seq", None),
        P("cb", None),
        P("cb", None, None, None),
        P("cb", None, None),
    )
    return jax.shard_map(
        shards,
        mesh=mesh,
        in_specs=placed,
        out_specs=(P(None, "seq", None), P(None, "seq", "cb", None)),
        check_vma=False,
    )
```

profile of v0, /device:TPU:0, one launch (start us, length us, event | category | flops | bytes accessed | tf_op | source)
XLA Modules:
  0.0 226.2 jit_solution(6674186344711236983)
XLA Ops:
  0.6 1.1 constant_dynamic-slice_fusion
  1.7 3.1 %collective-permute-start.3 = (bf16[512,512]{1,0:T(8,128)(2,1)S(1)}, bf16[512,512]{1,0:T(8,128)(2,1)S(1)}, u32[]{:S(2)}, u32[]{:S(2)}) collective-permute-start(bf16[512,512]{1,0:T(8,128)(2,1)S(1)} %constant_dynamic-slice_fusion), channel_id=1, source_target_pairs={{0,1},{1,2},{2,3},{3,0},{4,5},{5,6},{6,7},{7,4},{8,9},{9,10},{10,1... | collective-permute-start | bytes 1572872 | tf_op jit(solution)/shard_map/ppermute | solution.py:41
  4.8 13.9 %collective-permute-done.3 = bf16[512,512]{1,0:T(8,128)(2,1)S(1)} collective-permute-done((bf16[512,512]{1,0:T(8,128)(2,1)S(1)}, bf16[512,512]{1,0:T(8,128)(2,1)S(1)}, u32[]{:S(2)}, u32[]{:S(2)}) %collective-permute-start.3) | collective-permute-done | bytes 524320 | tf_op jit(solution)/shard_map/ppermute | solution.py:41
  18.8 10.8 %shard_map.113 = bf16[2,4,128,384]{3,2,1,0:T(8,128)(2,1)} custom-call(bf16[256,4096]{1,0:T(8,128)(2,1)} %bitcast.36, f32[1,4096]{1,0:T(1,128)} %bitcast.44, bf16[3,4096,512]{2,1,0:T(8,128)(2,1)} %weight_ref.1), custom_call_target="tpu_custom_call" | custom-call | flops 3221225472 | bytes 14680064 | tf_op jit(solution)/shard_map/pallas_call | solution.py:92
  29.5 4.2 %all-to-all-start = ((bf16[8,128,384]{2,1,0:T(8,128)(2,1)}), bf16[8,128,384]{2,1,0:T(8,128)(2,1)}, u32[]{:S(2)}, u32[]{:S(2)}) async-start(bf16[8,128,384]{2,1,0:T(8,128)(2,1)} %bitcast.40), calls=%async_computation | async-start | bytes 1572864 | tf_op jit(solution)/shard_map/all_to_all | solution.py:149
  33.9 2.0 collective-permute-start.22
  35.8 1.5 collective-permute-start.27
  38.0 1.1 collective-permute-start.5
  39.2 1.1 slice_bitcast_fusion.4
  40.2 6.7 %all-to-all-done = bf16[8,128,384]{2,1,0:T(8,128)(2,1)} async-done(((bf16[8,128,384]{2,1,0:T(8,128)(2,1)}), bf16[8,128,384]{2,1,0:T(8,128)(2,1)}, u32[]{:S(2)}, u32[]{:S(2)}) %all-to-all-start) | async-done | bytes 786464 | tf_op jit(solution)/shard_map/all_to_all | solution.py:149
  47.0 3.6 %shard_map.114 = bf16[1024,128]{1,0:T(8,128)(2,1)} custom-call(bf16[1024,384]{1,0:T(8,128)(2,1)} %bitcast.5.packed_ref), custom_call_target="tpu_custom_call" | custom-call | flops 402653184 | bytes 1048576 | tf_op jit(solution)/shard_map/pallas_call | solution.py:134
  50.6 3.4 %all-to-all-start.1 = ((bf16[8,128,128]{2,1,0:T(8,128)(2,1)}), bf16[8,128,128]{2,1,0:T(8,128)(2,1)S(1)}, u32[]{:S(2)}, u32[]{:S(2)}) async-start(bf16[8,128,128]{2,1,0:T(8,128)(2,1)} %bitcast.43), calls=%async_computation.1 | async-start | bytes 524288 | tf_op jit(solution)/shard_map/all_to_all | solution.py:151
  54.0 3.3 %collective-permute-done.22.refs_4_ = bf16[256,1024]{1,0:T(8,128)(2,1)} collective-permute-done((bf16[256,1024]{1,0:T(8,128)(2,1)S(1)}, bf16[256,1024]{1,0:T(8,128)(2,1)}, u32[]{:S(2)}, u32[]{:S(2)}) %collective-permute-start.22) | collective-permute-done | bytes 524320 | tf_op jit(solution)/shard_map/ppermute | solution.py:36
  57.8 10.6 %collective-permute-done.23.refs_5_ = bf16[256,1024]{1,0:T(8,128)(2,1)S(1)} collective-permute-done((bf16[256,1024]{1,0:T(8,128)(2,1)S(1)}, bf16[256,1024]{1,0:T(8,128)(2,1)S(1)}, u32[]{:S(2)}, u32[]{:S(2)}) %collective-permute-start.23) | collective-permute-done | bytes 524320 | tf_op jit(solution)/shard_map/ppermute | solution.py:36
  68.4 1.5 collective-permute-start.30
  70.5 1.1 slice_bitcast_fusion.3
  71.6 1.8 slice_bitcast_fusion.2
  73.5 1.2 collective-permute-start
  76.5 7.0 %collective-permute-done.30.refs_12_ = bf16[256,1024]{1,0:T(8,128)(2,1)} collective-permute-done((bf16[256,1024]{1,0:T(8,128)(2,1)}, bf16[256,1024]{1,0:T(8,128)(2,1)}, u32[]{:S(2)}, u32[]{:S(2)}) %collective-permute-start.30) | collective-permute-done | bytes 524320 | tf_op jit(solution)/shard_map/ppermute | solution.py:36
  83.5 1.3 collective-permute-done.31.refs_13_
  85.5 1.5 collective-permute-start.12
  87.0 2.2 collective-permute-start.1
  89.2 10.0 %collective-permute-done.1.refs_2_ = bf16[8,128,128]{2,1,0:T(8,128)(2,1)S(1)} collective-permute-done((bf16[8,128,128]{2,1,0:T(8,128)(2,1)S(1)}, bf16[8,128,128]{2,1,0:T(8,128)(2,1)S(1)}, u32[]{:S(2)}, u32[]{:S(2)}) %collective-permute-start.1) | collective-permute-done | bytes 262176 | tf_op jit(solution)/shard_map/ppermute | solution.py:41
  99.2 3.1 %collective-permute-start.2 = (bf16[8,128,128]{2,1,0:T(8,128)(2,1)S(1)}, bf16[8,128,128]{2,1,0:T(8,128)(2,1)}, u32[]{:S(2)}, u32[]{:S(2)}) collective-permute-start(bf16[8,128,128]{2,1,0:T(8,128)(2,1)S(1)} %all-to-all-done.1.refs_0_), channel_id=1, source_target_pairs={{0,3},{1,0},{2,1},{3,2},{4,7},{5,4},{6,5},{7,6},{8,11},{9,8},{10,9... | collective-permute-start | bytes 786440 | tf_op jit(solution)/shard_map/ppermute | solution.py:41
  102.2 5.0 %collective-permute-done.2.refs_3_ = bf16[8,128,128]{2,1,0:T(8,128)(2,1)} collective-permute-done((bf16[8,128,128]{2,1,0:T(8,128)(2,1)S(1)}, bf16[8,128,128]{2,1,0:T(8,128)(2,1)}, u32[]{:S(2)}, u32[]{:S(2)}) %collective-permute-start.2) | collective-permute-done | bytes 262176 | tf_op jit(solution)/shard_map/ppermute | solution.py:41
  107.7 2.3 %collective-permute-start.17 = (bf16[3,256,512]{2,1,0:T(8,128)(2,1)S(1)}, bf16[3,256,512]{2,1,0:T(8,128)(2,1)}, u32[]{:S(2)}, u32[]{:S(2)}) collective-permute-start(bf16[3,256,512]{2,1,0:T(8,128)(2,1)S(1)} %collective-permute-done.13.refs_14_), channel_id=1, source_target_pairs={{0,8},{4,12},{8,0},{12,4},{16,24},{20,28},{24,16},{28,20},{1,9},{5... | collective-permute-start | bytes 2359304 | tf_op jit(solution)/shard_map/ppermute | solution.py:36
  110.0 10.9 %collective-permute-done.9.refs_10_ = bf16[3,256,512]{2,1,0:T(8,128)(2,1)} collective-permute-done((bf16[3,256,512]{2,1,0:T(8,128)(2,1)S(1)}, bf16[3,256,512]{2,1,0:T(8,128)(2,1)}, u32[]{:S(2)}, u32[]{:S(2)}) %collective-permute-start.9) | collective-permute-done | bytes 786464 | tf_op jit(solution)/shard_map/ppermute | solution.py:36
  120.9 1.5 collective-permute-start.16
  123.0 12.1 %collective-permute-done.17.refs_18_ = bf16[3,256,512]{2,1,0:T(8,128)(2,1)} collective-permute-done((bf16[3,256,512]{2,1,0:T(8,128)(2,1)S(1)}, bf16[3,256,512]{2,1,0:T(8,128)(2,1)}, u32[]{:S(2)}, u32[]{:S(2)}) %collective-permute-start.17) | collective-permute-done | bytes 786464 | tf_op jit(solution)/shard_map/ppermute | solution.py:36
  137.3 4.3 %gather_fusion = bf16[256,1024]{1,0:T(8,128)(2,1)S(1)} fusion(bf16[2048,1024]{1,0:T(8,128)(2,1)} %bitcast.39, s32[1024]{0:T(1024)S(1)} %pad_clamp_fusion), kind=kCustom, calls=%fused_computation | custom fusion | bytes 1049600 | tf_op jit(solution)/shard_map/jit(_take)/gather | solution.py:468
  144.4 10.7 %shard_map.115.temporal_ref = bf16[256,4096]{1,0:T(8,128)(2,1)} custom-call(s32[2]{0:T(128)} %pad_add_fusion.place_ref, bf16[256,4096]{1,0:T(8,128)(2,1)} %bitcast.37, bf16[8,128,128]{2,1,0:T(8,128)(2,1)} %copy-done.4, bf16[8,128,128]{2,1,0:T(8,128)(2,1)} %copy-done.15, bf16[8,128,128]{2,1,0:T(8,128)(2,1)} %copy-done.16, ...), custom_call_target="tpu_custom_call" | custom-call | flops 4294967296 | bytes 16777216 | tf_op jit(solution)/shard_map/pallas_call | solution.py:232
  156.1 9.2 %shard_map.116 = (bf16[256,1024]{1,0:T(8,128)(2,1)}, bf16[256,1024]{1,0:T(8,128)(2,1)}, bf16[64,1536]{1,0:T(8,128)(2,1)}, bf16[64,1536]{1,0:T(8,128)(2,1)}, bf16...) custom-call(s32[2]{0:T(128)} %pad_add_fusion.place_ref, bf16[256,4096]{1,0:T(8,128)(2,1)} %shard_map.115.temporal_ref, ...), custom_call_target="tpu_custom_call" | custom-call | flops 2952790016 | bytes 11534336 | tf_op jit(solution)/shard_map/pallas_call | solution.py:311
  165.4 4.1 %shard_map.118 = (bf16[64,1536]{1,0:T(8,128)(2,1)}, bf16[64,1536]{1,0:T(8,128)(2,1)}, bf16[64,1536]{1,0:T(8,128)(2,1)}, bf16[64,1536]{1,0:T(8,128)(2,1)}) custom-call(s32[2]{0:T(128)} %pad_add_fusion.place_ref, bf16[256,1024]{1,0:T(8,128)(2,1)} %get-tuple-element.29.normed_ref, bf16[3,1024,1024]{2,1,0:T(8,128)(2,1)} %bitcast.35), custom_call_target="tpu_custom_call" | custom-call | flops 805306368 | bytes 3145728 | tf_op jit(solution)/shard_map/pallas_call | solution.py:338
  169.5 1.1 collective-permute-start.40
  170.6 3.1 %collective-permute-start.41 = (bf16[64,1536]{1,0:T(8,128)(2,1)}, bf16[64,1536]{1,0:T(8,128)(2,1)S(1)}, u32[]{:S(2)}, u32[]{:S(2)}) collective-permute-start(bf16[64,1536]{1,0:T(8,128)(2,1)} %get-tuple-element.32), channel_id=1, source_target_pairs={{0,2},{1,3},{2,0},{3,1},{4,6},{5,7},{6,4},{7,5},{8,10},{9,11},{10,... | collective-permute-start | bytes 589832 | tf_op jit(solution)/shard_map/ppermute | solution.py:41
  174.6 1.2 collective-permute-start.34
  175.7 3.7 %collective-permute-done.40.refs_1_ = bf16[64,1536]{1,0:T(8,128)(2,1)S(1)} collective-permute-done((bf16[64,1536]{1,0:T(8,128)(2,1)}, bf16[64,1536]{1,0:T(8,128)(2,1)S(1)}, u32[]{:S(2)}, u32[]{:S(2)}) %collective-permute-start.40) | collective-permute-done | bytes 196640 | tf_op jit(solution)/shard_map/ppermute | solution.py:41
  179.4 2.0 collective-permute-start.36
  181.4 6.4 %collective-permute-done.41.refs_2_ = bf16[64,1536]{1,0:T(8,128)(2,1)S(1)} collective-permute-done((bf16[64,1536]{1,0:T(8,128)(2,1)}, bf16[64,1536]{1,0:T(8,128)(2,1)S(1)}, u32[]{:S(2)}, u32[]{:S(2)}) %collective-permute-start.41) | collective-permute-done | bytes 196640 | tf_op jit(solution)/shard_map/ppermute | solution.py:41
  188.6 3.5 %shard_map.119 = (bf16[64,512]{1,0:T(8,128)(2,1)}, bf16[64,512]{1,0:T(8,128)(2,1)}, bf16[64,512]{1,0:T(8,128)(2,1)}, bf16[64,512]{1,0:T(8,128)(2,1)}) custom-call(s32[2]{0:T(128)} %pad_add_fusion.place_ref, bf16[64,1536]{1,0:T(8,128)(2,1)} %get-tuple-element.30.refs_0_, bf16[64,1536]{1,0:T(8,128)(2,1)} %copy-done.30, bf16[64,1536]{1,0:T(8,128)(2,1)} %copy-done.31, ...), custom_call_target="tpu_custom_call" | custom-call | flops 268435456 | bytes 1048576 | tf_op jit(solution)/shard_map/pallas_call | solution.py:396
  192.1 13.1 %collective-permute-start.43 = (bf16[64,512]{1,0:T(8,128)(2,1)}, bf16[64,512]{1,0:T(8,128)(2,1)S(1)}, u32[]{:S(2)}, u32[]{:S(2)}) collective-permute-start(bf16[64,512]{1,0:T(8,128)(2,1)} %get-tuple-element.35), channel_id=1, source_target_pairs={{0,1},{1,2},{2,3},{3,0},{4,5},{5,6},{6,7},{7,4},{8,9},{9,10},{10,1... | collective-permute-start | bytes 196616 | tf_op jit(solution)/shard_map/ppermute | solution.py:41
  205.2 1.2 collective-permute-start.44
  206.4 1.2 collective-permute-start.45
  208.3 3.5 %shard_map.117 = (bf16[64,512]{1,0:T(8,128)(2,1)}, bf16[64,512]{1,0:T(8,128)(2,1)}, bf16[64,512]{1,0:T(8,128)(2,1)}, bf16[64,512]{1,0:T(8,128)(2,1)}) custom-call(s32[2]{0:T(128)} %pad_add_fusion.place_ref, bf16[64,1536]{1,0:T(8,128)(2,1)} %get-tuple-element.21.refs_0_, bf16[64,1536]{1,0:T(8,128)(2,1)} %copy-done.27, bf16[64,1536]{1,0:T(8,128)(2,1)} %copy-done.28, ...), custom_call_target="tpu_custom_call" | custom-call | flops 268435456 | bytes 1048576 | tf_op jit(solution)/shard_map/pallas_call | solution.py:396
  211.8 4.2 %collective-permute-start.37 = (bf16[64,512]{1,0:T(8,128)(2,1)}, bf16[64,512]{1,0:T(8,128)(2,1)S(1)}, u32[]{:S(2)}, u32[]{:S(2)}) collective-permute-start(bf16[64,512]{1,0:T(8,128)(2,1)} %get-tuple-element.26), channel_id=1, source_target_pairs={{0,1},{1,2},{2,3},{3,0},{4,5},{5,6},{6,7},{7,4},{8,9},{9,10},{10,1... | collective-permute-start | bytes 196616 | tf_op jit(solution)/shard_map/ppermute | solution.py:41
  216.0 2.4 %collective-permute-start.39 = (bf16[64,512]{1,0:T(8,128)(2,1)}, bf16[64,512]{1,0:T(8,128)(2,1)S(1)}, u32[]{:S(2)}, u32[]{:S(2)}) collective-permute-start(bf16[64,512]{1,0:T(8,128)(2,1)} %get-tuple-element.28), channel_id=1, source_target_pairs={{0,3},{1,0},{2,1},{3,2},{4,7},{5,4},{6,5},{7,6},{8,11},{9,8},{10,9... | collective-permute-start | bytes 196616 | tf_op jit(solution)/shard_map/ppermute | solution.py:41
  218.5 3.7 %collective-permute-done.38.refs_2_ = bf16[64,512]{1,0:T(8,128)(2,1)S(1)} collective-permute-done((bf16[64,512]{1,0:T(8,128)(2,1)}, bf16[64,512]{1,0:T(8,128)(2,1)S(1)}, u32[]{:S(2)}, u32[]{:S(2)}) %collective-permute-start.38) | collective-permute-done | bytes 65568 | tf_op jit(solution)/shard_map/ppermute | solution.py:41
  222.9 3.3 %shard_map.120 = bf16[256,1024]{1,0:T(8,128)(2,1)} custom-call(s32[2]{0:T(128)} %pad_add_fusion.place_ref, bf16[256,1024]{1,0:T(8,128)(2,1)} %get-tuple-element.20.stream_ref, bf16[1024,1024]{1,0:T(8,128)(2,1)} %bitcast.41, bf16[64,512]{1,0:T(8,128)(2,1)} %get-tuple-element.25.refs_0_, bf16[64,512]{1,0:T(8,128)(2,1)} %copy-done.20, ...), custom_call_target="tpu_custom_call" | custom-call | flops 536870912 | bytes 2097152 | tf_op jit(solution)/shard_map/pallas_call | solution.py:426
  (135 shorter events, 14.6 us)
Async XLA Ops:
  1.7 17.1 %collective-permute-start.3 = (bf16[512,512]{1,0:T(8,128)(2,1)S(1)}, bf16[512,512]{1,0:T(8,128)(2,1)S(1)}, u32[]{:S(2)}, u32[]{:S(2)}) collective-permute-start(bf16[512,512]{1,0:T(8,128)(2,1)S(1)} %constant_dynamic-slice_fusion), channel_id=1, source_target_pairs={{0,1},{1,2},{2,3},{3,0},{4,5},{5,6},{6,7},{7,4},{8,9},{9,10},{10,1... | collective-permute-start | bytes 1572872 | tf_op jit(solution)/shard_map/ppermute | solution.py:41
  18.8 19.2 %collective-permute-start.4 = (bf16[512,512]{1,0:T(8,128)(2,1)S(1)}, bf16[512,512]{1,0:T(8,128)(2,1)}, u32[]{:S(2)}, u32[]{:S(2)}) collective-permute-start(bf16[512,512]{1,0:T(8,128)(2,1)S(1)} %collective-permute-done.3), channel_id=1, source_target_pairs={{0,1},{1,2},{2,3},{3,0},{4,5},{5,6},{6,7},{7,4},{8,9},{9,10},{10,1... | collective-permute-start | bytes 1572872 | tf_op jit(solution)/shard_map/ppermute | solution.py:41
  29.5 17.4 %all-to-all-start = ((bf16[8,128,384]{2,1,0:T(8,128)(2,1)}), bf16[8,128,384]{2,1,0:T(8,128)(2,1)}, u32[]{:S(2)}, u32[]{:S(2)}) async-start(bf16[8,128,384]{2,1,0:T(8,128)(2,1)} %bitcast.40), calls=%async_computation | async-start | bytes 1572864 | tf_op jit(solution)/shard_map/all_to_all | solution.py:149
  33.9 23.4 %collective-permute-start.22 = (bf16[256,1024]{1,0:T(8,128)(2,1)S(1)}, bf16[256,1024]{1,0:T(8,128)(2,1)}, u32[]{:S(2)}, u32[]{:S(2)}) collective-permute-start(bf16[256,1024]{1,0:T(8,128)(2,1)S(1)} %get-tuple-element.41.refs_0_), channel_id=1, source_target_pairs={{0,8},{4,12},{8,0},{12,4},{16,24},{20,28},{24,16},{28,20},{1,9},{5... | collective-permute-start | bytes 1572872 | tf_op jit(solution)/shard_map/ppermute | solution.py:36
  35.8 21.4 %collective-permute-start.27 = (bf16[256,1024]{1,0:T(8,128)(2,1)S(1)}, bf16[256,1024]{1,0:T(8,128)(2,1)}, u32[]{:S(2)}, u32[]{:S(2)}) collective-permute-start(bf16[256,1024]{1,0:T(8,128)(2,1)S(1)} %get-tuple-element.40.refs_1_), channel_id=1, source_target_pairs={{0,16},{4,20},{8,24},{12,28},{16,0},{20,4},{24,8},{28,12},{1,17},{... | collective-permute-start | bytes 1572872 | tf_op jit(solution)/shard_map/ppermute | solution.py:36
  37.3 31.1 %collective-permute-start.23 = (bf16[256,1024]{1,0:T(8,128)(2,1)S(1)}, bf16[256,1024]{1,0:T(8,128)(2,1)S(1)}, u32[]{:S(2)}, u32[]{:S(2)}) collective-permute-start(bf16[256,1024]{1,0:T(8,128)(2,1)S(1)} %get-tuple-element.40.refs_1_), channel_id=1, source_target_pairs={{0,8},{4,12},{8,0},{12,4},{16,24},{20,28},{24,16},{28,20},{1,9},{5... | collective-permute-start | bytes 1572872 | tf_op jit(solution)/shard_map/ppermute | solution.py:36
  37.9 32.0 %collective-permute-start.26 = (bf16[256,1024]{1,0:T(8,128)(2,1)S(1)}, bf16[256,1024]{1,0:T(8,128)(2,1)S(1)}, u32[]{:S(2)}, u32[]{:S(2)}) collective-permute-start(bf16[256,1024]{1,0:T(8,128)(2,1)S(1)} %get-tuple-element.41.refs_0_), channel_id=1, source_target_pairs={{0,16},{4,20},{8,24},{12,28},{16,0},{20,4},{24,8},{28,12},{1,17},{... | collective-permute-start | bytes 1572872 | tf_op jit(solution)/shard_map/ppermute | solution.py:36
  38.0 31.9 %collective-permute-start.5 = (bf16[512,512]{1,0:T(8,128)(2,1)}, bf16[512,512]{1,0:T(8,128)(2,1)}, u32[]{:S(2)}, u32[]{:S(2)}) collective-permute-start(bf16[512,512]{1,0:T(8,128)(2,1)} %collective-permute-done.4), channel_id=1, source_target_pairs={{0,1},{1,2},{2,3},{3,0},{4,5},{5,6},{6,7},{7,4},{8,9},{9,10},{10,1... | collective-permute-start | bytes 1572872 | tf_op jit(solution)/shard_map/ppermute | solution.py:41
  50.6 22.9 %all-to-all-start.1 = ((bf16[8,128,128]{2,1,0:T(8,128)(2,1)}), bf16[8,128,128]{2,1,0:T(8,128)(2,1)S(1)}, u32[]{:S(2)}, u32[]{:S(2)}) async-start(bf16[8,128,128]{2,1,0:T(8,128)(2,1)} %bitcast.43), calls=%async_computation.1 | async-start | bytes 524288 | tf_op jit(solution)/shard_map/all_to_all | solution.py:151
  57.3 16.2 %collective-permute-start.20 = (bf16[256,1024]{1,0:T(8,128)(2,1)S(1)}, bf16[256,1024]{1,0:T(8,128)(2,1)}, u32[]{:S(2)}, u32[]{:S(2)}) collective-permute-start(bf16[256,1024]{1,0:T(8,128)(2,1)S(1)} %get-tuple-element.41.refs_0_), channel_id=1, source_target_pairs={{0,4},{4,0},{8,12},{12,8},{16,20},{20,16},{24,28},{28,24},{1,5},{5... | collective-permute-start | bytes 1572872 | tf_op jit(solution)/shard_map/ppermute | solution.py:36
  57.3 18.4 %collective-permute-start.21 = (bf16[256,1024]{1,0:T(8,128)(2,1)S(1)}, bf16[256,1024]{1,0:T(8,128)(2,1)}, u32[]{:S(2)}, u32[]{:S(2)}) collective-permute-start(bf16[256,1024]{1,0:T(8,128)(2,1)S(1)} %get-tuple-element.40.refs_1_), channel_id=1, source_target_pairs={{0,4},{4,0},{8,12},{12,8},{16,20},{20,16},{24,28},{28,24},{1,5},{5... | collective-permute-start | bytes 1572872 | tf_op jit(solution)/shard_map/ppermute | solution.py:36
  68.4 15.1 %collective-permute-start.30 = (bf16[256,1024]{1,0:T(8,128)(2,1)}, bf16[256,1024]{1,0:T(8,128)(2,1)}, u32[]{:S(2)}, u32[]{:S(2)}) collective-permute-start(bf16[256,1024]{1,0:T(8,128)(2,1)} %collective-permute-done.22.refs_4_), channel_id=1, source_target_pairs={{0,16},{4,20},{8,24},{12,28},{16,0},{20,4},{24,8},{28,12},{1,17},{... | collective-permute-start | bytes 1572872 | tf_op jit(solution)/shard_map/ppermute | solution.py:36
  69.9 15.6 %collective-permute-start.24 = (bf16[256,1024]{1,0:T(8,128)(2,1)}, bf16[256,1024]{1,0:T(8,128)(2,1)}, u32[]{:S(2)}, u32[]{:S(2)}) collective-permute-start(bf16[256,1024]{1,0:T(8,128)(2,1)} %collective-permute-done.22.refs_4_), channel_id=1, source_target_pairs={{0,4},{4,0},{8,12},{12,8},{16,20},{20,16},{24,28},{28,24},{1,5},{5... | collective-permute-start | bytes 1572872 | tf_op jit(solution)/shard_map/ppermute | solution.py:36
  69.9 14.9 %collective-permute-start.31 = (bf16[256,1024]{1,0:T(8,128)(2,1)}, bf16[256,1024]{1,0:T(8,128)(2,1)}, u32[]{:S(2)}, u32[]{:S(2)}) collective-permute-start(bf16[256,1024]{1,0:T(8,128)(2,1)} %collective-permute-done.27.refs_9_), channel_id=1, source_target_pairs={{0,8},{4,12},{8,0},{12,4},{16,24},{20,28},{24,16},{28,20},{1,9},{5... | collective-permute-start | bytes 1572872 | tf_op jit(solution)/shard_map/ppermute | solution.py:36
  73.5 13.6 %collective-permute-start = (bf16[8,128,128]{2,1,0:T(8,128)(2,1)S(1)}, bf16[8,128,128]{2,1,0:T(8,128)(2,1)S(1)}, u32[]{:S(2)}, u32[]{:S(2)}) collective-permute-start(bf16[8,128,128]{2,1,0:T(8,128)(2,1)S(1)} %all-to-all-done.1.refs_0_), channel_id=1, source_target_pairs={{0,1},{1,2},{2,3},{3,0},{4,5},{5,6},{6,7},{7,4},{8,9},{9,10},{10,1... | collective-permute-start | bytes 786440 | tf_op jit(solution)/shard_map/ppermute | solution.py:41
  75.7 31.5 %collective-permute-start.13 = (bf16[3,256,512]{2,1,0:T(8,128)(2,1)S(1)}, bf16[3,256,512]{2,1,0:T(8,128)(2,1)S(1)}, u32[]{:S(2)}, u32[]{:S(2)}) collective-permute-start(bf16[3,256,512]{2,1,0:T(8,128)(2,1)S(1)} %pad_maximum_fusion.1.refs_6_), channel_id=1, source_target_pairs={{0,16},{4,20},{8,24},{12,28},{16,0},{20,4},{24,8},{28,12},{1,17},{... | collective-permute-start | bytes 2359304 | tf_op jit(solution)/shard_map/ppermute | solution.py:36
  83.5 24.2 %collective-permute-start.8 = (bf16[3,256,512]{2,1,0:T(8,128)(2,1)S(1)}, bf16[3,256,512]{2,1,0:T(8,128)(2,1)}, u32[]{:S(2)}, u32[]{:S(2)}) collective-permute-start(bf16[3,256,512]{2,1,0:T(8,128)(2,1)S(1)} %pad_maximum_fusion.refs_5_), channel_id=1, source_target_pairs={{0,8},{4,12},{8,0},{12,4},{16,24},{20,28},{24,16},{28,20},{1,9},{5... | collective-permute-start | bytes 2359304 | tf_op jit(solution)/shard_map/ppermute | solution.py:36
  84.8 36.1 %collective-permute-start.9 = (bf16[3,256,512]{2,1,0:T(8,128)(2,1)S(1)}, bf16[3,256,512]{2,1,0:T(8,128)(2,1)}, u32[]{:S(2)}, u32[]{:S(2)}) collective-permute-start(bf16[3,256,512]{2,1,0:T(8,128)(2,1)S(1)} %pad_maximum_fusion.1.refs_6_), channel_id=1, source_target_pairs={{0,8},{4,12},{8,0},{12,4},{16,24},{20,28},{24,16},{28,20},{1,9},{5... | collective-permute-start | bytes 2359304 | tf_op jit(solution)/shard_map/ppermute | solution.py:36
  85.5 36.8 %collective-permute-start.12 = (bf16[3,256,512]{2,1,0:T(8,128)(2,1)S(1)}, bf16[3,256,512]{2,1,0:T(8,128)(2,1)}, u32[]{:S(2)}, u32[]{:S(2)}) collective-permute-start(bf16[3,256,512]{2,1,0:T(8,128)(2,1)S(1)} %pad_maximum_fusion.refs_5_), channel_id=1, source_target_pairs={{0,16},{4,20},{8,24},{12,28},{16,0},{20,4},{24,8},{28,12},{1,17},{... | collective-permute-start | bytes 2359304 | tf_op jit(solution)/shard_map/ppermute | solution.py:36
  87.0 12.1 %collective-permute-start.1 = (bf16[8,128,128]{2,1,0:T(8,128)(2,1)S(1)}, bf16[8,128,128]{2,1,0:T(8,128)(2,1)S(1)}, u32[]{:S(2)}, u32[]{:S(2)}) collective-permute-start(bf16[8,128,128]{2,1,0:T(8,128)(2,1)S(1)} %all-to-all-done.1.refs_0_), channel_id=1, source_target_pairs={{0,2},{1,3},{2,0},{3,1},{4,6},{5,7},{6,4},{7,5},{8,10},{9,11},{10,... | collective-permute-start | bytes 786440 | tf_op jit(solution)/shard_map/ppermute | solution.py:41
  99.2 8.0 %collective-permute-start.2 = (bf16[8,128,128]{2,1,0:T(8,128)(2,1)S(1)}, bf16[8,128,128]{2,1,0:T(8,128)(2,1)}, u32[]{:S(2)}, u32[]{:S(2)}) collective-permute-start(bf16[8,128,128]{2,1,0:T(8,128)(2,1)S(1)} %all-to-all-done.1.refs_0_), channel_id=1, source_target_pairs={{0,3},{1,0},{2,1},{3,2},{4,7},{5,4},{6,5},{7,6},{8,11},{9,8},{10,9... | collective-permute-start | bytes 786440 | tf_op jit(solution)/shard_map/ppermute | solution.py:41
  107.2 15.2 %collective-permute-start.7 = (bf16[3,256,512]{2,1,0:T(8,128)(2,1)S(1)}, bf16[3,256,512]{2,1,0:T(8,128)(2,1)S(1)}, u32[]{:S(2)}, u32[]{:S(2)}) collective-permute-start(bf16[3,256,512]{2,1,0:T(8,128)(2,1)S(1)} %pad_maximum_fusion.1.refs_6_), channel_id=1, source_target_pairs={{0,4},{4,0},{8,12},{12,8},{16,20},{20,16},{24,28},{28,24},{1,5},{5... | collective-permute-start | bytes 2359304 | tf_op jit(solution)/shard_map/ppermute | solution.py:36
  107.2 15.7 %collective-permute-start.6 = (bf16[3,256,512]{2,1,0:T(8,128)(2,1)S(1)}, bf16[3,256,512]{2,1,0:T(8,128)(2,1)S(1)}, u32[]{:S(2)}, u32[]{:S(2)}) collective-permute-start(bf16[3,256,512]{2,1,0:T(8,128)(2,1)S(1)} %pad_maximum_fusion.refs_5_), channel_id=1, source_target_pairs={{0,4},{4,0},{8,12},{12,8},{16,20},{20,16},{24,28},{28,24},{1,5},{5... | collective-permute-start | bytes 2359304 | tf_op jit(solution)/shard_map/ppermute | solution.py:36
  107.7 27.4 %collective-permute-start.17 = (bf16[3,256,512]{2,1,0:T(8,128)(2,1)S(1)}, bf16[3,256,512]{2,1,0:T(8,128)(2,1)}, u32[]{:S(2)}, u32[]{:S(2)}) collective-permute-start(bf16[3,256,512]{2,1,0:T(8,128)(2,1)S(1)} %collective-permute-done.13.refs_14_), channel_id=1, source_target_pairs={{0,8},{4,12},{8,0},{12,4},{16,24},{20,28},{24,16},{28,20},{1,9},{5... | collective-permute-start | bytes 2359304 | tf_op jit(solution)/shard_map/ppermute | solution.py:36
  120.9 14.9 %collective-permute-start.16 = (bf16[3,256,512]{2,1,0:T(8,128)(2,1)}, bf16[3,256,512]{2,1,0:T(8,128)(2,1)}, u32[]{:S(2)}, u32[]{:S(2)}) collective-permute-start(bf16[3,256,512]{2,1,0:T(8,128)(2,1)} %collective-permute-done.8.refs_9_), channel_id=1, source_target_pairs={{0,16},{4,20},{8,24},{12,28},{16,0},{20,4},{24,8},{28,12},{1,17},{... | collective-permute-start | bytes 2359304 | tf_op jit(solution)/shard_map/ppermute | solution.py:36
  122.4 13.4 %collective-permute-start.15 = (bf16[3,256,512]{2,1,0:T(8,128)(2,1)S(1)}, bf16[3,256,512]{2,1,0:T(8,128)(2,1)S(1)}, u32[]{:S(2)}, u32[]{:S(2)}) collective-permute-start(bf16[3,256,512]{2,1,0:T(8,128)(2,1)S(1)} %collective-permute-done.13.refs_14_), channel_id=1, source_target_pairs={{0,4},{4,0},{8,12},{12,8},{16,20},{20,16},{24,28},{28,24},{1,5},{5... | collective-permute-start | bytes 2359304 | tf_op jit(solution)/shard_map/ppermute | solution.py:36
  122.4 19.2 %collective-permute-start.10 = (bf16[3,256,512]{2,1,0:T(8,128)(2,1)}, bf16[3,256,512]{2,1,0:T(8,128)(2,1)}, u32[]{:S(2)}, u32[]{:S(2)}) collective-permute-start(bf16[3,256,512]{2,1,0:T(8,128)(2,1)} %collective-permute-done.8.refs_9_), channel_id=1, source_target_pairs={{0,4},{4,0},{8,12},{12,8},{16,20},{20,16},{24,28},{28,24},{1,5},{5... | collective-permute-start | bytes 2359304 | tf_op jit(solution)/shard_map/ppermute | solution.py:36
  122.9 18.8 %collective-permute-start.11 = (bf16[3,256,512]{2,1,0:T(8,128)(2,1)}, bf16[3,256,512]{2,1,0:T(8,128)(2,1)}, u32[]{:S(2)}, u32[]{:S(2)}) collective-permute-start(bf16[3,256,512]{2,1,0:T(8,128)(2,1)} %collective-permute-done.9.refs_10_), channel_id=1, source_target_pairs={{0,4},{4,0},{8,12},{12,8},{16,20},{20,16},{24,28},{28,24},{1,5},{5... | collective-permute-start | bytes 2359304 | tf_op jit(solution)/shard_map/ppermute | solution.py:36
  135.1 7.1 %collective-permute-start.14 = (bf16[3,256,512]{2,1,0:T(8,128)(2,1)}, bf16[3,256,512]{2,1,0:T(8,128)(2,1)}, u32[]{:S(2)}, u32[]{:S(2)}) collective-permute-start(bf16[3,256,512]{2,1,0:T(8,128)(2,1)} %collective-permute-done.12.refs_13_), channel_id=1, source_target_pairs={{0,4},{4,0},{8,12},{12,8},{16,20},{20,16},{24,28},{28,24},{1,5},{5... | collective-permute-start | bytes 2359304 | tf_op jit(solution)/shard_map/ppermute | solution.py:36
  135.8 6.5 %collective-permute-start.19 = (bf16[3,256,512]{2,1,0:T(8,128)(2,1)}, bf16[3,256,512]{2,1,0:T(8,128)(2,1)}, u32[]{:S(2)}, u32[]{:S(2)}) collective-permute-start(bf16[3,256,512]{2,1,0:T(8,128)(2,1)} %collective-permute-done.17.refs_18_), channel_id=1, source_target_pairs={{0,4},{4,0},{8,12},{12,8},{16,20},{20,16},{24,28},{28,24},{1,5},{5... | collective-permute-start | bytes 2359304 | tf_op jit(solution)/shard_map/ppermute | solution.py:36
  136.8 6.0 %collective-permute-start.18 = (bf16[3,256,512]{2,1,0:T(8,128)(2,1)}, bf16[3,256,512]{2,1,0:T(8,128)(2,1)}, u32[]{:S(2)}, u32[]{:S(2)}) collective-permute-start(bf16[3,256,512]{2,1,0:T(8,128)(2,1)} %collective-permute-done.16.refs_17_), channel_id=1, source_target_pairs={{0,4},{4,0},{8,12},{12,8},{16,20},{20,16},{24,28},{28,24},{1,5},{5... | collective-permute-start | bytes 2359304 | tf_op jit(solution)/shard_map/ppermute | solution.py:36
  141.6 13.5 %collective-permute-start.29 = (bf16[256,1024]{1,0:T(8,128)(2,1)}, bf16[256,1024]{1,0:T(8,128)(2,1)S(1)}, u32[]{:S(2)}, u32[]{:S(2)}) collective-permute-start(bf16[256,1024]{1,0:T(8,128)(2,1)} %collective-permute-done.27.refs_9_), channel_id=1, source_target_pairs={{0,4},{4,0},{8,12},{12,8},{16,20},{20,16},{24,28},{28,24},{1,5},{5... | collective-permute-start | bytes 1572872 | tf_op jit(solution)/shard_map/ppermute | solution.py:36
  141.7 13.4 %collective-permute-start.25 = (bf16[256,1024]{1,0:T(8,128)(2,1)}, bf16[256,1024]{1,0:T(8,128)(2,1)S(1)}, u32[]{:S(2)}, u32[]{:S(2)}) collective-permute-start(bf16[256,1024]{1,0:T(8,128)(2,1)} %copy-done.10), channel_id=1, source_target_pairs={{0,4},{4,0},{8,12},{12,8},{16,20},{20,16},{24,28},{28,24},{1,5},{5... | collective-permute-start | bytes 1572872 | tf_op jit(solution)/shard_map/ppermute | solution.py:36
  142.2 12.9 %collective-permute-start.28 = (bf16[256,1024]{1,0:T(8,128)(2,1)}, bf16[256,1024]{1,0:T(8,128)(2,1)}, u32[]{:S(2)}, u32[]{:S(2)}) collective-permute-start(bf16[256,1024]{1,0:T(8,128)(2,1)} %copy-done.11), channel_id=1, source_target_pairs={{0,4},{4,0},{8,12},{12,8},{16,20},{20,16},{24,28},{28,24},{1,5},{5... | collective-permute-start | bytes 1572872 | tf_op jit(solution)/shard_map/ppermute | solution.py:36
  142.3 12.9 %collective-permute-start.32 = (bf16[256,1024]{1,0:T(8,128)(2,1)}, bf16[256,1024]{1,0:T(8,128)(2,1)}, u32[]{:S(2)}, u32[]{:S(2)}) collective-permute-start(bf16[256,1024]{1,0:T(8,128)(2,1)} %collective-permute-done.30.refs_12_), channel_id=1, source_target_pairs={{0,4},{4,0},{8,12},{12,8},{16,20},{20,16},{24,28},{28,24},{1,5},{5... | collective-permute-start | bytes 1572872 | tf_op jit(solution)/shard_map/ppermute | solution.py:36
  142.7 12.4 %collective-permute-start.33 = (bf16[256,1024]{1,0:T(8,128)(2,1)}, bf16[256,1024]{1,0:T(8,128)(2,1)}, u32[]{:S(2)}, u32[]{:S(2)}) collective-permute-start(bf16[256,1024]{1,0:T(8,128)(2,1)} %collective-permute-done.31.refs_13_), channel_id=1, source_target_pairs={{0,4},{4,0},{8,12},{12,8},{16,20},{20,16},{24,28},{28,24},{1,5},{5... | collective-permute-start | bytes 1572872 | tf_op jit(solution)/shard_map/ppermute | solution.py:36
  169.5 9.9 %collective-permute-start.40 = (bf16[64,1536]{1,0:T(8,128)(2,1)}, bf16[64,1536]{1,0:T(8,128)(2,1)S(1)}, u32[]{:S(2)}, u32[]{:S(2)}) collective-permute-start(bf16[64,1536]{1,0:T(8,128)(2,1)} %get-tuple-element.31), channel_id=1, source_target_pairs={{0,1},{1,2},{2,3},{3,0},{4,5},{5,6},{6,7},{7,4},{8,9},{9,10},{10,1... | collective-permute-start | bytes 589832 | tf_op jit(solution)/shard_map/ppermute | solution.py:41
  170.6 17.2 %collective-permute-start.41 = (bf16[64,1536]{1,0:T(8,128)(2,1)}, bf16[64,1536]{1,0:T(8,128)(2,1)S(1)}, u32[]{:S(2)}, u32[]{:S(2)}) collective-permute-start(bf16[64,1536]{1,0:T(8,128)(2,1)} %get-tuple-element.32), channel_id=1, source_target_pairs={{0,2},{1,3},{2,0},{3,1},{4,6},{5,7},{6,4},{7,5},{8,10},{9,11},{10,... | collective-permute-start | bytes 589832 | tf_op jit(solution)/shard_map/ppermute | solution.py:41
  173.7 14.1 %collective-permute-start.42 = (bf16[64,1536]{1,0:T(8,128)(2,1)}, bf16[64,1536]{1,0:T(8,128)(2,1)S(1)}, u32[]{:S(2)}, u32[]{:S(2)}) collective-permute-start(bf16[64,1536]{1,0:T(8,128)(2,1)} %get-tuple-element.33), channel_id=1, source_target_pairs={{0,3},{1,0},{2,1},{3,2},{4,7},{5,4},{6,5},{7,6},{8,11},{9,8},{10,9... | collective-permute-start | bytes 589832 | tf_op jit(solution)/shard_map/ppermute | solution.py:41
  174.6 31.8 %collective-permute-start.34 = (bf16[64,1536]{1,0:T(8,128)(2,1)S(1)}, bf16[64,1536]{1,0:T(8,128)(2,1)S(1)}, u32[]{:S(2)}, u32[]{:S(2)}) collective-permute-start(bf16[64,1536]{1,0:T(8,128)(2,1)S(1)} %copy-done.26), channel_id=1, source_target_pairs={{0,1},{1,2},{2,3},{3,0},{4,5},{5,6},{6,7},{7,4},{8,9},{9,10},{10,1... | collective-permute-start | bytes 589832 | tf_op jit(solution)/shard_map/ppermute | solution.py:41
  175.7 31.8 %collective-permute-start.35 = (bf16[64,1536]{1,0:T(8,128)(2,1)S(1)}, bf16[64,1536]{1,0:T(8,128)(2,1)S(1)}, u32[]{:S(2)}, u32[]{:S(2)}) collective-permute-start(bf16[64,1536]{1,0:T(8,128)(2,1)S(1)} %copy-done.25), channel_id=1, source_target_pairs={{0,2},{1,3},{2,0},{3,1},{4,6},{5,7},{6,4},{7,5},{8,10},{9,11},{10,... | collective-permute-start | bytes 589832 | tf_op jit(solution)/shard_map/ppermute | solution.py:41
  179.4 28.2 %collective-permute-start.36 = (bf16[64,1536]{1,0:T(8,128)(2,1)S(1)}, bf16[64,1536]{1,0:T(8,128)(2,1)S(1)}, u32[]{:S(2)}, u32[]{:S(2)}) collective-permute-start(bf16[64,1536]{1,0:T(8,128)(2,1)S(1)} %copy-done.24), channel_id=1, source_target_pairs={{0,3},{1,0},{2,1},{3,2},{4,7},{5,4},{6,5},{7,6},{8,11},{9,8},{10,9... | collective-permute-start | bytes 589832 | tf_op jit(solution)/shard_map/ppermute | solution.py:41
  192.1 23.9 %collective-permute-start.43 = (bf16[64,512]{1,0:T(8,128)(2,1)}, bf16[64,512]{1,0:T(8,128)(2,1)S(1)}, u32[]{:S(2)}, u32[]{:S(2)}) collective-permute-start(bf16[64,512]{1,0:T(8,128)(2,1)} %get-tuple-element.35), channel_id=1, source_target_pairs={{0,1},{1,2},{2,3},{3,0},{4,5},{5,6},{6,7},{7,4},{8,9},{9,10},{10,1... | collective-permute-start | bytes 196616 | tf_op jit(solution)/shard_map/ppermute | solution.py:41
  205.2 13.2 %collective-permute-start.44 = (bf16[64,512]{1,0:T(8,128)(2,1)}, bf16[64,512]{1,0:T(8,128)(2,1)S(1)}, u32[]{:S(2)}, u32[]{:S(2)}) collective-permute-start(bf16[64,512]{1,0:T(8,128)(2,1)} %get-tuple-element.36), channel_id=1, source_target_pairs={{0,2},{1,3},{2,0},{3,1},{4,6},{5,7},{6,4},{7,5},{8,10},{9,11},{10,... | collective-permute-start | bytes 196616 | tf_op jit(solution)/shard_map/ppermute | solution.py:41
  206.4 12.0 %collective-permute-start.45 = (bf16[64,512]{1,0:T(8,128)(2,1)}, bf16[64,512]{1,0:T(8,128)(2,1)S(1)}, u32[]{:S(2)}, u32[]{:S(2)}) collective-permute-start(bf16[64,512]{1,0:T(8,128)(2,1)} %get-tuple-element.37), channel_id=1, source_target_pairs={{0,3},{1,0},{2,1},{3,2},{4,7},{5,4},{6,5},{7,6},{8,11},{9,8},{10,9... | collective-permute-start | bytes 196616 | tf_op jit(solution)/shard_map/ppermute | solution.py:41
  211.8 6.7 %collective-permute-start.37 = (bf16[64,512]{1,0:T(8,128)(2,1)}, bf16[64,512]{1,0:T(8,128)(2,1)S(1)}, u32[]{:S(2)}, u32[]{:S(2)}) collective-permute-start(bf16[64,512]{1,0:T(8,128)(2,1)} %get-tuple-element.26), channel_id=1, source_target_pairs={{0,1},{1,2},{2,3},{3,0},{4,5},{5,6},{6,7},{7,4},{8,9},{9,10},{10,1... | collective-permute-start | bytes 196616 | tf_op jit(solution)/shard_map/ppermute | solution.py:41
  216.0 6.3 %collective-permute-start.38 = (bf16[64,512]{1,0:T(8,128)(2,1)}, bf16[64,512]{1,0:T(8,128)(2,1)S(1)}, u32[]{:S(2)}, u32[]{:S(2)}) collective-permute-start(bf16[64,512]{1,0:T(8,128)(2,1)} %get-tuple-element.27), channel_id=1, source_target_pairs={{0,2},{1,3},{2,0},{3,1},{4,6},{5,7},{6,4},{7,5},{8,10},{9,11},{10,... | collective-permute-start | bytes 196616 | tf_op jit(solution)/shard_map/ppermute | solution.py:41
  216.0 6.3 %collective-permute-start.39 = (bf16[64,512]{1,0:T(8,128)(2,1)}, bf16[64,512]{1,0:T(8,128)(2,1)S(1)}, u32[]{:S(2)}, u32[]{:S(2)}) collective-permute-start(bf16[64,512]{1,0:T(8,128)(2,1)} %get-tuple-element.28), channel_id=1, source_target_pairs={{0,3},{1,0},{2,1},{3,2},{4,7},{5,4},{6,5},{7,6},{8,11},{9,8},{10,9... | collective-permute-start | bytes 196616 | tf_op jit(solution)/shard_map/ppermute | solution.py:41
  (33 other events, 723.4 us)
where the time goes:
time: 227 us; the launch traced here: 226 us
  waiting for transfers between devices  95.5 us (42%)
  starting transfers between devices  64.9 us (29%)
  Pallas kernels  48.6 us (21%)
  local copies, waits for them, and re-layouts  13.3 us (6%)
  other arithmetic  2.71 us (1%)
    ppermute x28, waiting for transfers between devices, flip(): lax.ppermute(x, axis, [(i, i ^ bit) for i in range(lax.axis_size(axis))])  45.9 us
    ppermute x18, waiting for transfers between devices, shift(): return lax.ppermute(x, axis, [(i, (i + by) % size) for i in range(size)])  42.9 us
    ppermute x18, starting transfers between devices, shift(): return lax.ppermute(x, axis, [(i, (i + by) % size) for i in range(size)])  41 us
    ppermute x28, starting transfers between devices, flip(): lax.ppermute(x, axis, [(i, i ^ bit) for i in range(lax.axis_size(axis))])  16.3 us
    pallas_call x1, Pallas kernels, project(): pl.pallas_call(project_body, grid=(3 * parts,), in_specs=[pl.BlockSpec((r...  10.8 us
    pallas_call x1, Pallas kernels, temporal_output(): pl.pallas_call(body, in_specs=[SM, VM] + [VM] * groups + [ANY] * (1 + 2 *...  10.7 us
    pallas_call x1, Pallas kernels, stream_kernel(): pl.pallas_call(body, in_specs=[SM, VM, VM, VM, ANY] + [ANY] * (2 * size),...  9.24 us
    pallas_call x2, Pallas kernels, depth_attention(): pl.pallas_call(body, in_specs=[SM] + [VM] * books, out_specs=[VM] * books...  6.92 us
  transfers between devices with their start and end apart: 48, of which 15 were waited for; matrix products, arithmetic and copies ran while one was open for 5% of the time, Pallas kernels for 14%

commit v1 on v0

--- a/solution.py
+++ b/solution.py
@@ -15,7 +15,9 @@
 F32 = jnp.float32
 BF16 = jnp.bfloat16
 CHUNKS = 2
-VMEM_LIMIT = 60 * 1024 * 1024
+VMEM_LIMIT = 32 * 1024 * 1024
+EARLY_LIMIT = 40 * 1024 * 1024
+LATE_LIMIT = 32 * 1024 * 1024
 
 
 VM = pl.BlockSpec(memory_space=pltpu.VMEM)
@@ -166,82 +168,124 @@
     return (mixed / totals).astype(BF16).reshape(pairs, frames, HD)
 
 
-def output_body(place_ref, hidden_ref, *refs):
-    books = place_ref.shape[0] - 2
-    del books
-    mixed_refs, (own_ref,), pieces, (out_ref, cat_ref, weight_ref, sems) = refs
-    size, groups, _, half, block = weight_ref.shape
-    seqs_heads, frames, _ = mixed_refs[0].shape
-    cols = 2 * half
+def put_mixed(mixed_refs, cat_ref):
+    pairs, frames, _ = mixed_refs[0].shape
+    cols = cat_ref.shape[1] // len(mixed_refs)
     heads = cols // HD
-    me = place_ref[0]
-
-    def copies(at):
-        column = pl.multiple_of((me ^ at) * block, block)
-        found = []
-        for side in range(2):
-            found.append(
-                pltpu.make_async_copy(
-                    own_ref.at[side * half : (side + 1) * half, pl.ds(column, block)],
-                    weight_ref.at[at, 0, side],
-                    sems.at[at, side],
-                )
-            )
-            found.append(
-                pltpu.make_async_copy(
-                    pieces[2 * at + side], weight_ref.at[at, 1:, side], sems.at[at, 2 + side]
-                )
-            )
-        return found
-
-    for at in range(size):
-        for copy in copies(at):
-            copy.start()
-    for group in range(groups):
-        for pair in range(seqs_heads):
+    for group, ref in enumerate(mixed_refs):
+        for pair in range(pairs):
             s, h = pair // heads, pair % heads
-            cat_ref[s * frames : (s + 1) * frames, group * cols + h * HD : group * cols + (h + 1) * HD] = (
-                mixed_refs[group][pair]
-            )
-    for at in range(size):
-        for copy in copies(at):
-            copy.wait()
-        span = pl.ds(pl.multiple_of((me ^ at) * block, block), block)
-        summed = dot(cat_ref[...], weight_ref[at].reshape(groups * cols, block))
-        out_ref[:, span] = (hidden_ref[:, span].astype(F32) + summed).astype(BF16)
-
-
-def temporal_output(place, hidden, mixed, own, pieces):
+            at = group * cols + h * HD
+            cat_ref[s * frames : (s + 1) * frames, at : at + HD] = ref[pair]
+
+
+def chip_start(me, at, wide):
+    return pl.multiple_of(lax.shift_right_logical(me ^ at, 1) * wide, wide)
+
+
+def early_output(place, hidden, mixed, own, out_pieces, in_pieces, late):
     rows, width = hidden.shape
     cols = own.shape[0]
     groups = len(mixed)
-    size = len(pieces) // 2
+    size = len(out_pieces) // 2
     block = width // size
+    half, deep = in_pieces[0].shape
+    chips = [at for at in range(0, size, 2) if at != late]
+    count = len(chips)
+    used = [2 * (at + core) + side for at in chips for core in range(2) for side in range(2)]
 
     def body(place_ref, hidden_ref, *refs):
-        refs = list(refs)
-        output_body(
-            place_ref,
-            hidden_ref,
-            refs[:groups],
-            refs[groups : groups + 1],
-            refs[groups + 1 : groups + 1 + 2 * size],
-            refs[groups + 1 + 2 * size :],
-        )
+        mixed_refs = refs[:groups]
+        own_ref = refs[groups]
+        outs = refs[groups + 1 : groups + 1 + 4 * count]
+        ins = refs[groups + 1 + 4 * count : groups + 1 + 8 * count]
+        out_ref, acc_ref, cat_ref, out_buf, in_buf, out_sems, in_sems = refs[groups + 1 + 8 * count :]
+        me = place_ref[0]
+
+        def out_copies(index):
+            at = chips[index // 2] + index % 2
+            column = pl.multiple_of((me ^ at) * block, block)
+            found = []
+            for side in range(2):
+                found.append(
+                    pltpu.make_async_copy(
+                        own_ref.at[side * (cols // 2) : (side + 1) * (cols // 2), pl.ds(column, block)],
+                        out_buf.at[index, 0, side],
+                        out_sems.at[index, side],
+                    )
+                )
+                found.append(
+                    pltpu.make_async_copy(
+                        outs[2 * index + side], out_buf.at[index, 1:, side], out_sems.at[index, 2 + side]
+                    )
+                )
+            return found
+
+        def in_copies(chip):
+            found = []
+            for core in range(2):
+                where = (me ^ core) & 1
+                for side in range(2):
+                    found.append(
+                        pltpu.make_async_copy(
+                            ins[4 * chip + 2 * core + side],
+                            in_buf.at[chip, where, side],
+                            in_sems.at[chip, 2 * core + side],
+                        )
+                    )
+            return found
+
+        for index in range(2 * count):
+            for copy in out_copies(index):
+                copy.start()
+        for chip in range(count):
+            for copy in in_copies(chip):
+                copy.start()
+        put_mixed(mixed_refs, cat_ref)
+        for index in range(2 * count):
+            at = chips[index // 2] + index % 2
+            for copy in out_copies(index):
+                copy.wait()
+            span = pl.ds(pl.multiple_of((me ^ at) * block, block), block)
+            summed = dot(cat_ref[...], out_buf[index].reshape(groups * cols, block))
+            out_ref[:, span] = (hidden_ref[:, span].astype(F32) + summed).astype(BF16)
+        for chip in range(count):
+            for copy in in_copies(chip):
+                copy.wait()
+            span = pl.ds(chip_start(me, chips[chip], 4 * half), 4 * half)
+            term = dot(out_ref[:, span], in_buf[chip].reshape(4 * half, deep))
+            if chip == 0:
+                acc_ref[...] = term
+            else:
+                acc_ref[...] += term
 
     return pl.pallas_call(
         body,
-        in_specs=[SM, VM] + [VM] * groups + [ANY] * (1 + 2 * size),
-        out_specs=VM,
-        out_shape=jax.ShapeDtypeStruct((rows, width), BF16),
+        in_specs=[SM, VM] + [VM] * groups + [ANY] * (1 + 8 * count),
+        out_specs=[VM, VM],
+        out_shape=[
+            jax.ShapeDtypeStruct((rows, width), BF16),
+            jax.ShapeDtypeStruct((rows, deep), F32),
+        ],
         scratch_shapes=[
             pltpu.VMEM((rows, groups * cols), BF16),
-            pltpu.VMEM((size, groups, 2, cols // 2, block), BF16),
-            pltpu.SemaphoreType.DMA((size, 4)),
+            pltpu.VMEM((2 * count, groups, 2, cols // 2, block), BF16),
+            pltpu.VMEM((count, 2, 2, half, deep), BF16),
+            pltpu.SemaphoreType.DMA((2 * count, 4)),
+            pltpu.SemaphoreType.DMA((count, 4)),
         ],
-        compiler_params=PARAMS,
-        cost_estimate=cost(2 * rows * groups * cols * width, 2 * groups * cols * width),
-    )(place, hidden, *mixed, own, *pieces)
+        compiler_params=pltpu.CompilerParams(vmem_limit_bytes=EARLY_LIMIT),
+        cost_estimate=cost(
+            2 * rows * width * (groups * cols + deep), 2 * width * (groups * cols + deep)
+        ),
+    )(
+        place,
+        hidden,
+        *mixed,
+        own,
+        *[out_pieces[i] for i in used],
+        *[in_pieces[i] for i in used],
+    )
 
 
 def put_qkv(normed, weights, out_refs, full_ref, book):
@@ -255,76 +299,92 @@
         out_refs[at][...] = full_ref[pl.ds(row, block), :].astype(BF16)
 
 
-def stream_kernel(place, temporal, pieces, entry, gain, weights, books, chunks):
-    rows, width = temporal.shape
-    size = len(pieces) // 2
-    half, deep = pieces[0].shape
-    block = rows // books
-    cols = deep // chunks
-    chips = size // 2
-
-    def body(place_ref, temporal_ref, entry_ref, gain_ref, qkv_ref, *refs):
-        piece_refs = refs[: 2 * size]
-        stream_ref, normed_ref = refs[2 * size : 2 * size + 2]
-        out_refs = refs[2 * size + 2 : 2 * size + 2 + books]
-        weight_ref, qkv_buf, acc_ref, full_ref, sems, qkv_sem = refs[2 * size + 2 + books :]
+def late_output(place, early, acc, hidden, mixed, own, out_pieces, in_pieces, entry, gain, weights, late, chunks):
+    rows, width = hidden.shape
+    books = len(mixed)
+    size = len(out_pieces) // 2
+    cols = own.shape[0]
+    block = width // size
+    half, deep = in_pieces[0].shape
+    part = deep // chunks
+    share = rows // books
+    used = [2 * (late + core) + side for core in range(2) for side in range(2)]
+
+    def body(place_ref, _, acc_ref, hidden_ref, entry_ref, gain_ref, own_ref, qkv_ref, *refs):
+        mixed_refs = refs[:books]
+        outs = refs[books : books + 4]
+        ins = refs[books + 4 : books + 8]
+        out_ref, stream_ref, normed_ref = refs[books + 8 : books + 11]
+        out_refs = refs[books + 11 : 2 * books + 11]
+        cat_ref, own_buf, qkv_buf, full_ref, late_buf, sems = refs[2 * books + 11 :]
         me = place_ref[0]
         book = place_ref[1]
-
-        def copies(chip):
-            found = []
-            for core in range(2):
-                at = 2 * chip + core
-                where = (me ^ at) & 1
-                for side in range(2):
-                    found.append(
-                        pltpu.make_async_copy(
-                            piece_refs[2 * at + side],
-                            weight_ref.at[chip, where, side],
-                            sems.at[chip, 2 * core + side],
-                        )
-                    )
-            return found
-
-        fetch = pltpu.make_async_copy(qkv_ref.at[:, :, 0:cols], qkv_buf, qkv_sem.at[0])
-        for chip in range(chips):
-            for copy in copies(chip):
-                copy.start()
-        fetch.start()
-        for chip in range(chips):
-            for copy in copies(chip):
-                copy.wait()
-            start = pl.multiple_of(lax.shift_right_logical(me ^ (2 * chip), 1) * 4 * half, 4 * half)
-            term = dot(temporal_ref[:, pl.ds(start, 4 * half)], weight_ref[chip].reshape(4 * half, deep))
-            if chip == 0:
-                acc_ref[...] = term
-            else:
-                acc_ref[...] += term
-        stream = (acc_ref[...] + entry_ref[...].astype(F32)).astype(BF16)
+        start = chip_start(me, late, 2 * block)
+        fetch_own = pltpu.make_async_copy(own_ref.at[:, pl.ds(start, 2 * block)], own_buf, sems.at[0])
+        fetch_qkv = pltpu.make_async_copy(qkv_ref.at[:, :, 0:part], qkv_buf, sems.at[1])
+        fetch_own.start()
+        fetch_qkv.start()
+        put_mixed(mixed_refs, cat_ref)
+        fetch_own.wait()
+        total = acc_ref[...] + entry_ref[...].astype(F32)
+        for core in range(2):
+            column = pl.multiple_of((me ^ (late + core)) * block, block)
+            span = pl.ds(column, block)
+            local = pl.ds(pl.multiple_of(((me ^ core) & 1) * block, block), block)
+            summed = dot(cat_ref[:, :cols], own_buf[:, local])
+            for side in range(2):
+                for group in range(1, books):
+                    at = group * cols + side * (cols // 2)
+                    summed += dot(cat_ref[:, at : at + cols // 2], outs[2 * core + side][group - 1])
+            value = (hidden_ref[:, span].astype(F32) + summed).astype(BF16)
+            late_buf[:, local] = value
+            for side in range(2):
+                total += dot(value[:, side * half : (side + 1) * half], ins[2 * core + side][...])
+        put = pltpu.make_async_copy(late_buf, out_ref.at[:, pl.ds(start, 2 * block)], sems.at[2])
+        put.start()
+        stream = total.astype(BF16)
         stream_ref[...] = stream
         values = stream.astype(F32)
         mean_sq = jnp.mean(values * values, axis=-1, keepdims=True)
         normed_ref[...] = (values * lax.rsqrt(mean_sq + EPS) * gain_ref[...]).astype(BF16)
-        fetch.wait()
+        fetch_qkv.wait()
         put_qkv(normed_ref[...], qkv_buf, out_refs, full_ref, book)
+        put.wait()
 
     return pl.pallas_call(
         body,
-        in_specs=[SM, VM, VM, VM, ANY] + [ANY] * (2 * size),
-        out_specs=[VM] * (2 + books),
-        out_shape=[jax.ShapeDtypeStruct((rows, deep), BF16)] * 2
-        + [jax.ShapeDtypeStruct((block, 3 * cols), BF16)] * books,
+        in_specs=[SM, ANY, VM, VM, VM, VM, ANY, ANY] + [VM] * (books + 8),
+        out_specs=[ANY] + [VM] * (2 + books),
+        out_shape=[jax.ShapeDtypeStruct((rows, width), BF16)]
+        + [jax.ShapeDtypeStruct((rows, deep), BF16)] * 2
+        + [jax.ShapeDtypeStruct((share, 3 * part), BF16)] * books,
+        input_output_aliases={1: 0},
         scratch_shapes=[
-            pltpu.VMEM((chips, 2, 2, half, deep), BF16),
-            pltpu.VMEM((3, deep, cols), BF16),
-            pltpu.VMEM((rows, deep), F32),
-            pltpu.VMEM((rows, 3 * cols), F32),
-            pltpu.SemaphoreType.DMA((chips, 4)),
-            pltpu.SemaphoreType.DMA((1,)),
+            pltpu.VMEM((rows, books * cols), BF16),
+            pltpu.VMEM((cols, 2 * block), BF16),
+            pltpu.VMEM((3, deep, part), BF16),
+            pltpu.VMEM((rows, 3 * part), F32),
+            pltpu.VMEM((rows, 2 * block), BF16),
+            pltpu.SemaphoreType.DMA((3,)),
         ],
-        compiler_params=PARAMS,
-        cost_estimate=cost(2 * rows * width * deep + 6 * rows * deep * cols, 2 * width * deep + 6 * deep * cols),
-    )(place, temporal, entry, gain, weights, *pieces)
+        compiler_params=pltpu.CompilerParams(vmem_limit_bytes=LATE_LIMIT),
+        cost_estimate=cost(
+            rows * width * (books * cols + deep) // 2 + 6 * rows * deep * part,
+            width * (books * cols + deep) // 2 + 6 * deep * part,
+        ),
+    )(
+        place,
+        early,
+        acc,
+        hidden,
+        entry,
+        gain,
+        own,
+        weights,
+        *mixed,
+        *[out_pieces[i] for i in used],
+        *[in_pieces[i] for i in used],
+    )
 
 
 def qkv_kernel(place, normed, weights, books, part, chunks):
@@ -452,8 +512,8 @@
     cols = temporal_out.shape[0]
     size = lax.axis_size("seq")
     books = lax.axis_size("cb")
+
     place = jnp.stack([lax.axis_index("seq"), lax.axis_index("cb")]).astype(jnp.int32)
-
     block = width // size
     ring = [lax.dynamic_slice_in_dim(temporal_out, lax.axis_index("seq") * block, block, 1)]
     for _ in range(1, books):
@@ -470,10 +530,13 @@
     packed = project(hidden, temporal_gain, temporal_qkv)
     own_mixed = temporal_attention(packed)
     mixed = [own_mixed] + [shift(own_mixed, "cb", by) for by in range(1, books)]
-    temporal = temporal_output(
-        place, hidden.reshape(rows, width), mixed, temporal_out, out_pieces
+    late = size - 2
+    flat = hidden.reshape(rows, width)
+    early, acc = early_output(place, flat, mixed, temporal_out, out_pieces, in_pieces, late)
+    temporal, stream, normed, *sent = late_output(
+        place, early, acc, flat, mixed, temporal_out, out_pieces, in_pieces,
+        entry, depth_gain, depth_qkv[0], late, CHUNKS,
     )
-    stream, normed, *sent = stream_kernel(place, temporal, in_pieces, entry, depth_gain, depth_qkv[0], books, CHUNKS)
     arrived, returned = [], []
     for part in range(CHUNKS):
         if part > 0:

time: 227 us -> 244 us (1.075)
  local copies, waits for them, and re-layouts: 13.3 us -> 42.7 us
  blocking collectives: 0 us -> 28.6 us
  waiting for transfers between devices: 95.5 us -> 77.8 us
  Pallas kernels: 48.6 us -> 33.1 us
  starting transfers between devices: 64.9 us -> 58.2 us
    all_to_all x0 -> x1, blocking collectives: none -> 28.6 us  [temporal_attention(): lax.all_to_all(mixed.reshape(size, frames, HD), 'seq', split_axis=0, conc...]
    unnamed x66 -> x78, local copies, waits for them, and re-layouts: 4.01 us -> 30.9 us
    ppermute x28, waiting for transfers between devices: 45.9 us -> 25.3 us  [flip(): lax.ppermute(x, axis, [(i, i ^ bit) for i in range(lax.axis_size(axis))])]
    ppermute x18, waiting for transfers between devices: 42.9 us -> 51.9 us  [shift(): return lax.ppermute(x, axis, [(i, (i + by) % size) for i in range(size)])]
    all_to_all x1, waiting for transfers between devices: 6.74 us -> 0.64 us  [temporal_attention(): lax.all_to_all(packed.reshape(pairs, frames, 3 * HD), 'seq', split_axis=0...]
    pallas_call x1, Pallas kernels: 10.8 us -> 7.06 us  [project(): pl.pallas_call(project_body, grid=(3 * parts,), in_specs=[pl.BlockSpec((r...]
    pallas_call x2, Pallas kernels: 19.9 us -> 16.5 us  [the longest x1 10.2 us: early_output(): pl.pallas_call(body, in_specs=[SM, VM] + [VM] * groups + [ANY] * (1 + 8 *...]
    all_to_all x1 -> x0, starting transfers between devices: 3.41 us -> none  [temporal_attention(): lax.all_to_all(mixed.reshape(size, frames, HD), 'seq', split_axis=0, conc...]
  transfers between devices with their start and end apart: 48 -> 47, of which waited for: 15 -> 12; matrix products, arithmetic and copies ran while one was open for 5% -> 5% of each run, Pallas kernels for 14% -> 10%
where the time goes in v1:
time: 244 us; the launch traced here: 243 us
  waiting for transfers between devices  77.8 us (32%)
  starting transfers between devices  58.2 us (24%)
  local copies, waits for them, and re-layouts  42.7 us (18%)
  Pallas kernels  33.1 us (14%)
  blocking collectives  28.6 us (12%)
    ppermute x18, waiting for transfers between devices, shift(): return lax.ppermute(x, axis, [(i, (i + by) % size) for i in range(size)])  51.9 us
    ppermute x18, starting transfers between devices, shift(): return lax.ppermute(x, axis, [(i, (i + by) % size) for i in range(size)])  39.4 us
    unnamed x78, local copies, waits for them, and re-layouts  30.9 us
    all_to_all x1, blocking collectives, temporal_attention(): lax.all_to_all(mixed.reshape(size, frames, HD), 'seq', split_axis=0, conc...  28.6 us
    ppermute x28, waiting for transfers between devices, flip(): lax.ppermute(x, axis, [(i, i ^ bit) for i in range(lax.axis_size(axis))])  25.3 us
    ppermute x28, starting transfers between devices, flip(): lax.ppermute(x, axis, [(i, i ^ bit) for i in range(lax.axis_size(axis))])  15.3 us
    pallas_call x1, Pallas kernels, early_output(): pl.pallas_call(body, in_specs=[SM, VM] + [VM] * groups + [ANY] * (1 + 8 *...  10.2 us
    pallas_call x1, Pallas kernels, project(): pl.pallas_call(project_body, grid=(3 * parts,), in_specs=[pl.BlockSpec((r...  7.06 us
  transfers between devices with their start and end apart: 47, of which 12 were waited for; matrix products, arithmetic and copies ran while one was open for 5% of the time, Pallas kernels for 10%

profile of v1, /device:TPU:0, one launch (start us, length us, event | category | flops | bytes accessed | tf_op | source)
XLA Modules:
  0.0 243.0 jit_solution(6086972013815587837)
XLA Ops:
  0.6 1.2 constant_dynamic-slice_fusion
  1.9 3.1 %collective-permute-start.3 = (bf16[512,512]{1,0:T(8,128)(2,1)S(1)}, bf16[512,512]{1,0:T(8,128)(2,1)S(1)}, u32[]{:S(2)}, u32[]{:S(2)}) collective-permute-start(bf16[512,512]{1,0:T(8,128)(2,1)S(1)} %constant_dynamic-slice_fusion), channel_id=1, source_target_pairs={{0,1},{1,2},{2,3},{3,0},{4,5},{5,6},{6,7},{7,4},{8,9},{9,10},{10,1... | collective-permute-start | bytes 1572872 | tf_op jit(solution)/shard_map/ppermute | solution.py:43
  5.0 13.9 %collective-permute-done.3 = bf16[512,512]{1,0:T(8,128)(2,1)S(1)} collective-permute-done((bf16[512,512]{1,0:T(8,128)(2,1)S(1)}, bf16[512,512]{1,0:T(8,128)(2,1)S(1)}, u32[]{:S(2)}, u32[]{:S(2)}) %collective-permute-start.3) | collective-permute-done | bytes 524320 | tf_op jit(solution)/shard_map/ppermute | solution.py:43
  18.9 2.3 slice_bitcast_fusion
  21.2 1.5 collective-permute-start.23
  22.7 1.5 collective-permute-start.19
  25.2 8.7 %collective-permute-done.4 = bf16[512,512]{1,0:T(8,128)(2,1)} collective-permute-done((bf16[512,512]{1,0:T(8,128)(2,1)S(1)}, bf16[512,512]{1,0:T(8,128)(2,1)}, u32[]{:S(2)}, u32[]{:S(2)}) %collective-permute-start.4) | collective-permute-done | bytes 524320 | tf_op jit(solution)/shard_map/ppermute | solution.py:43
  33.9 4.6 %copy-done = bf16[3,4096,512]{2,1,0:T(8,128)(2,1)S(1)} copy-done((bf16[3,4096,512]{2,1,0:T(8,128)(2,1)S(1)}, bf16[3,4096,512]{2,1,0:T(8,128)(2,1)}, u32[]{:S(2)}) %copy-start) | copy-done | bytes 12582936
  39.2 7.1 %shard_map.113 = bf16[2,4,128,384]{3,2,1,0:T(8,128)(2,1)} custom-call(bf16[256,4096]{1,0:T(8,128)(2,1)S(1)} %bitcast.39, f32[1,4096]{1,0:T(1,128)S(1)} %bitcast.44, bf16[3,4096,512]{2,1,0:T(8,128)(2,1)S(1)} %copy-done), custom_call_target="tpu_custom_call" | custom-call | flops 3221225472 | bytes 14680064 | tf_op jit(solution)/shard_map/pallas_call | solution.py:94
  46.3 3.5 %all-to-all-start = ((bf16[8,128,384]{2,1,0:T(8,128)(2,1)}), bf16[8,128,384]{2,1,0:T(8,128)(2,1)S(1)}, u32[]{:S(2)}, u32[]{:S(2)}) async-start(bf16[8,128,384]{2,1,0:T(8,128)(2,1)} %bitcast.4), calls=%async_computation | async-start | bytes 1572864 | tf_op jit(solution)/shard_map/all_to_all | solution.py:151
  49.9 1.1 slice_bitcast_fusion.4
  53.6 1.1 slice_bitcast_fusion.2
  55.6 1.6 collective-permute-start.30
  58.0 1.5 collective-permute-start.31
  63.0 1.7 shard_map.114
  64.7 28.6 %all_to_all.10.refs_0_ = bf16[8,128,128]{2,1,0:T(8,128)(2,1)S(1)} all-to-all(bf16[8,128,128]{2,1,0:T(8,128)(2,1)S(1)} %bitcast.43), channel_id=1, replica_groups=mesh['seq'=8,'cb'=4] {'seq'}, dimensions={0} | all-to-all | bytes 524288 | tf_op jit(solution)/shard_map/all_to_all | solution.py:153
  93.3 4.4 %collective-permute-start.1 = (bf16[8,128,128]{2,1,0:T(8,128)(2,1)S(1)}, bf16[8,128,128]{2,1,0:T(8,128)(2,1)S(1)}, u32[]{:S(2)}, u32[]{:S(2)}) collective-permute-start(bf16[8,128,128]{2,1,0:T(8,128)(2,1)S(1)} %all_to_all.10.refs_0_), channel_id=1, source_target_pairs={{0,2},{1,3},{2,0},{3,1},{4,6},{5,7},{6,4},{7,5},{8,10},{9,11},{10,... | collective-permute-start | bytes 786440 | tf_op jit(solution)/shard_map/ppermute | solution.py:43
  97.7 6.7 %collective-permute-done.refs_1_ = bf16[8,128,128]{2,1,0:T(8,128)(2,1)S(1)} collective-permute-done((bf16[8,128,128]{2,1,0:T(8,128)(2,1)S(1)}, bf16[8,128,128]{2,1,0:T(8,128)(2,1)S(1)}, u32[]{:S(2)}, u32[]{:S(2)}) %collective-permute-start) | collective-permute-done | bytes 262176 | tf_op jit(solution)/shard_map/ppermute | solution.py:43
  105.6 8.6 %collective-permute-done.1.refs_2_ = bf16[8,128,128]{2,1,0:T(8,128)(2,1)S(1)} collective-permute-done((bf16[8,128,128]{2,1,0:T(8,128)(2,1)S(1)}, bf16[8,128,128]{2,1,0:T(8,128)(2,1)S(1)}, u32[]{:S(2)}, u32[]{:S(2)}) %collective-permute-start.1) | collective-permute-done | bytes 262176 | tf_op jit(solution)/shard_map/ppermute | solution.py:43
  116.8 5.4 %collective-permute-done.9.refs_10_ = bf16[3,256,512]{2,1,0:T(8,128)(2,1)} collective-permute-done((bf16[3,256,512]{2,1,0:T(8,128)(2,1)S(1)}, bf16[3,256,512]{2,1,0:T(8,128)(2,1)}, u32[]{:S(2)}, u32[]{:S(2)}) %collective-permute-start.9) | collective-permute-done | bytes 786464 | tf_op jit(solution)/shard_map/ppermute | solution.py:38
  122.2 1.7 collective-permute-start.27
  124.0 10.5 %collective-permute-done.12.refs_13_ = bf16[3,256,512]{2,1,0:T(8,128)(2,1)} collective-permute-done((bf16[3,256,512]{2,1,0:T(8,128)(2,1)S(1)}, bf16[3,256,512]{2,1,0:T(8,128)(2,1)}, u32[]{:S(2)}, u32[]{:S(2)}) %collective-permute-start.12) | collective-permute-done | bytes 786464 | tf_op jit(solution)/shard_map/ppermute | solution.py:38
  138.2 5.1 %gather_fusion = bf16[256,1024]{1,0:T(8,128)(2,1)} fusion(bf16[2048,1024]{1,0:T(8,128)(2,1)} %bitcast.45, s32[1024]{0:T(1024)S(1)} %pad_clamp_fusion), kind=kCustom, calls=%fused_computation | custom fusion | bytes 1049600 | tf_op jit(solution)/shard_map/jit(_take)/gather | solution.py:528
  144.0 9.3 %collective-permute-done.26.refs_4_ = bf16[3,256,512]{2,1,0:T(8,128)(2,1)} collective-permute-done((bf16[3,256,512]{2,1,0:T(8,128)(2,1)}, bf16[3,256,512]{2,1,0:T(8,128)(2,1)}, u32[]{:S(2)}, u32[]{:S(2)}) %collective-permute-start.26) | collective-permute-done | bytes 786464 | tf_op jit(solution)/shard_map/ppermute | solution.py:38
  153.3 1.3 broadcast_select_fusion.entry_ref
  155.3 1.5 copy-done.7
  156.8 1.1 copy-done.9
  161.8 1.1 copy-done.21
  163.0 1.1 copy-done.23
  169.3 10.2 %shard_map.115 = (bf16[256,4096]{1,0:T(8,128)(2,1)}, f32[256,1024]{1,0:T(8,128)}) custom-call(s32[2]{0:T(128)S(1)} %pad_add_fusion.place_ref, bf16[256,4096]{1,0:T(8,128)(2,1)} %bitcast.38, bf16[8,128,128]{2,1,0:T(8,128)(2,1)S(1)} %all_to_all.10.refs_0_, bf16[8,128,128]{2,1,0:T(8,128)(2,1)S(1)} %copy-done.13, bf16[8,128,128]{2,1,0:T(8,128)(2,1)S(1)} %copy-done.15, ...), custom_call_target="tpu_custom_call" | custom-call | flops 6442450944 | bytes 25165824 | tf_op jit(solution)/shard_map/pallas_call | solution.py:262
  179.6 2.2 copy-done.3
  181.8 1.2 copy-done.5
  183.0 6.3 %shard_map.116 = (bf16[256,4096]{1,0:T(8,128)(2,1)}, bf16[256,1024]{1,0:T(8,128)(2,1)S(1)}, bf16[256,1024]{1,0:T(8,128)(2,1)S(1)}, bf16[64,1536]{1,0:T(8,128)(2,...) custom-call(s32[2]{0:T(128)S(1)} %pad_add_fusion.place_ref, ...), custom_call_target="tpu_custom_call", output_to_operand_aliasing={{0}: (1, {})} | custom-call | flops 2415919104 | bytes 9437184 | tf_op jit(solution)/shard_map/pallas_call | solution.py:354
  189.3 1.6 shard_map.118
  191.0 2.3 collective-permute-start.41
  193.3 1.5 collective-permute-start.42
  195.4 1.5 collective-permute-start.35
  196.9 3.9 %collective-permute-done.40.refs_1_ = bf16[64,1536]{1,0:T(8,128)(2,1)S(1)} collective-permute-done((bf16[64,1536]{1,0:T(8,128)(2,1)S(1)}, bf16[64,1536]{1,0:T(8,128)(2,1)S(1)}, u32[]{:S(2)}, u32[]{:S(2)}) %collective-permute-start.40) | collective-permute-done | bytes 196640 | tf_op jit(solution)/shard_map/ppermute | solution.py:43
  200.7 1.7 collective-permute-start.36
  202.4 6.2 %collective-permute-done.41.refs_2_ = bf16[64,1536]{1,0:T(8,128)(2,1)S(1)} collective-permute-done((bf16[64,1536]{1,0:T(8,128)(2,1)S(1)}, bf16[64,1536]{1,0:T(8,128)(2,1)S(1)}, u32[]{:S(2)}, u32[]{:S(2)}) %collective-permute-start.41) | collective-permute-done | bytes 196640 | tf_op jit(solution)/shard_map/ppermute | solution.py:43
  208.7 2.1 shard_map.119
  210.8 13.2 %collective-permute-start.43 = (bf16[64,512]{1,0:T(8,128)(2,1)S(1)}, bf16[64,512]{1,0:T(8,128)(2,1)S(1)}, u32[]{:S(2)}, u32[]{:S(2)}) collective-permute-start(bf16[64,512]{1,0:T(8,128)(2,1)S(1)} %get-tuple-element.41), channel_id=1, source_target_pairs={{0,1},{1,2},{2,3},{3,0},{4,5},{5,6},{6,7},{7,4},{8,9},{9,10},{10,1... | collective-permute-start | bytes 196616 | tf_op jit(solution)/shard_map/ppermute | solution.py:43
  224.0 2.4 %collective-permute-start.45 = (bf16[64,512]{1,0:T(8,128)(2,1)S(1)}, bf16[64,512]{1,0:T(8,128)(2,1)S(1)}, u32[]{:S(2)}, u32[]{:S(2)}) collective-permute-start(bf16[64,512]{1,0:T(8,128)(2,1)S(1)} %get-tuple-element.43), channel_id=1, source_target_pairs={{0,3},{1,0},{2,1},{3,2},{4,7},{5,4},{6,5},{7,6},{8,11},{9,8},{10,9... | collective-permute-start | bytes 196616 | tf_op jit(solution)/shard_map/ppermute | solution.py:43
  227.2 2.1 shard_map.117
  229.3 6.2 %collective-permute-start.37 = (bf16[64,512]{1,0:T(8,128)(2,1)S(1)}, bf16[64,512]{1,0:T(8,128)(2,1)S(1)}, u32[]{:S(2)}, u32[]{:S(2)}) collective-permute-start(bf16[64,512]{1,0:T(8,128)(2,1)S(1)} %get-tuple-element.32), channel_id=1, source_target_pairs={{0,1},{1,2},{2,3},{3,0},{4,5},{5,6},{6,7},{7,4},{8,9},{9,10},{10,1... | collective-permute-start | bytes 196616 | tf_op jit(solution)/shard_map/ppermute | solution.py:43
  235.6 2.4 %collective-permute-start.39 = (bf16[64,512]{1,0:T(8,128)(2,1)S(1)}, bf16[64,512]{1,0:T(8,128)(2,1)S(1)}, u32[]{:S(2)}, u32[]{:S(2)}) collective-permute-start(bf16[64,512]{1,0:T(8,128)(2,1)S(1)} %get-tuple-element.34), channel_id=1, source_target_pairs={{0,3},{1,0},{2,1},{3,2},{4,7},{5,4},{6,5},{7,6},{8,11},{9,8},{10,9... | collective-permute-start | bytes 196616 | tf_op jit(solution)/shard_map/ppermute | solution.py:43
  238.0 2.9 %collective-permute-done.38.refs_2_ = bf16[64,512]{1,0:T(8,128)(2,1)S(1)} collective-permute-done((bf16[64,512]{1,0:T(8,128)(2,1)S(1)}, bf16[64,512]{1,0:T(8,128)(2,1)S(1)}, u32[]{:S(2)}, u32[]{:S(2)}) %collective-permute-start.38) | collective-permute-done | bytes 65568 | tf_op jit(solution)/shard_map/ppermute | solution.py:43
  240.9 2.1 shard_map.120
  (147 shorter events, 29.0 us)
Async XLA Ops:
  1.9 17.1 %collective-permute-start.3 = (bf16[512,512]{1,0:T(8,128)(2,1)S(1)}, bf16[512,512]{1,0:T(8,128)(2,1)S(1)}, u32[]{:S(2)}, u32[]{:S(2)}) collective-permute-start(bf16[512,512]{1,0:T(8,128)(2,1)S(1)} %constant_dynamic-slice_fusion), channel_id=1, source_target_pairs={{0,1},{1,2},{2,3},{3,0},{4,5},{5,6},{6,7},{7,4},{8,9},{9,10},{10,1... | collective-permute-start | bytes 1572872 | tf_op jit(solution)/shard_map/ppermute | solution.py:43
  18.9 15.0 %collective-permute-start.4 = (bf16[512,512]{1,0:T(8,128)(2,1)S(1)}, bf16[512,512]{1,0:T(8,128)(2,1)}, u32[]{:S(2)}, u32[]{:S(2)}) collective-permute-start(bf16[512,512]{1,0:T(8,128)(2,1)S(1)} %collective-permute-done.3), channel_id=1, source_target_pairs={{0,1},{1,2},{2,3},{3,0},{4,5},{5,6},{6,7},{7,4},{8,9},{9,10},{10,1... | collective-permute-start | bytes 1572872 | tf_op jit(solution)/shard_map/ppermute | solution.py:43
  21.2 30.3 %collective-permute-start.23 = (bf16[256,1024]{1,0:T(8,128)(2,1)}, bf16[256,1024]{1,0:T(8,128)(2,1)}, u32[]{:S(2)}, u32[]{:S(2)}) collective-permute-start(bf16[256,1024]{1,0:T(8,128)(2,1)} %get-tuple-element.46.refs_18_), channel_id=1, source_target_pairs={{0,16},{4,20},{8,24},{12,28},{16,0},{20,4},{24,8},{28,12},{1,17},{... | collective-permute-start | bytes 1572872 | tf_op jit(solution)/shard_map/ppermute | solution.py:38
  22.7 28.9 %collective-permute-start.19 = (bf16[256,1024]{1,0:T(8,128)(2,1)}, bf16[256,1024]{1,0:T(8,128)(2,1)}, u32[]{:S(2)}, u32[]{:S(2)}) collective-permute-start(bf16[256,1024]{1,0:T(8,128)(2,1)} %get-tuple-element.46.refs_18_), channel_id=1, source_target_pairs={{0,8},{4,12},{8,0},{12,4},{16,24},{20,28},{24,16},{28,20},{1,9},{5... | collective-permute-start | bytes 1572872 | tf_op jit(solution)/shard_map/ppermute | solution.py:38
  24.2 26.7 %collective-permute-start.18 = (bf16[256,1024]{1,0:T(8,128)(2,1)S(1)}, bf16[256,1024]{1,0:T(8,128)(2,1)}, u32[]{:S(2)}, u32[]{:S(2)}) collective-permute-start(bf16[256,1024]{1,0:T(8,128)(2,1)S(1)} %get-tuple-element.47.refs_17_), channel_id=1, source_target_pairs={{0,8},{4,12},{8,0},{12,4},{16,24},{20,28},{24,16},{28,20},{1,9},{5... | collective-permute-start | bytes 1572872 | tf_op jit(solution)/shard_map/ppermute | solution.py:38
  24.7 27.3 %collective-permute-start.22 = (bf16[256,1024]{1,0:T(8,128)(2,1)S(1)}, bf16[256,1024]{1,0:T(8,128)(2,1)}, u32[]{:S(2)}, u32[]{:S(2)}) collective-permute-start(bf16[256,1024]{1,0:T(8,128)(2,1)S(1)} %get-tuple-element.47.refs_17_), channel_id=1, source_target_pairs={{0,16},{4,20},{8,24},{12,28},{16,0},{20,4},{24,8},{28,12},{1,17},{... | collective-permute-start | bytes 1572872 | tf_op jit(solution)/shard_map/ppermute | solution.py:38
  33.9 18.2 %collective-permute-start.5 = (bf16[512,512]{1,0:T(8,128)(2,1)}, bf16[512,512]{1,0:T(8,128)(2,1)}, u32[]{:S(2)}, u32[]{:S(2)}) collective-permute-start(bf16[512,512]{1,0:T(8,128)(2,1)} %collective-permute-done.4), channel_id=1, source_target_pairs={{0,1},{1,2},{2,3},{3,0},{4,5},{5,6},{6,7},{7,4},{8,9},{9,10},{10,1... | collective-permute-start | bytes 1572872 | tf_op jit(solution)/shard_map/ppermute | solution.py:43
  46.3 16.7 %all-to-all-start = ((bf16[8,128,384]{2,1,0:T(8,128)(2,1)}), bf16[8,128,384]{2,1,0:T(8,128)(2,1)S(1)}, u32[]{:S(2)}, u32[]{:S(2)}) async-start(bf16[8,128,384]{2,1,0:T(8,128)(2,1)} %bitcast.4), calls=%async_computation | async-start | bytes 1572864 | tf_op jit(solution)/shard_map/all_to_all | solution.py:151
  51.0 3.8 %collective-permute-start.16 = (bf16[256,1024]{1,0:T(8,128)(2,1)S(1)}, bf16[256,1024]{1,0:T(8,128)(2,1)S(1)}, u32[]{:S(2)}, u32[]{:S(2)}) collective-permute-start(bf16[256,1024]{1,0:T(8,128)(2,1)S(1)} %get-tuple-element.47.refs_17_), channel_id=1, source_target_pairs={{0,4},{4,0},{8,12},{12,8},{16,20},{20,16},{24,28},{28,24},{1,5},{5... | collective-permute-start | bytes 1572872 | tf_op jit(solution)/shard_map/ppermute | solution.py:38
  51.5 5.8 %collective-permute-start.17 = (bf16[256,1024]{1,0:T(8,128)(2,1)}, bf16[256,1024]{1,0:T(8,128)(2,1)S(1)}, u32[]{:S(2)}, u32[]{:S(2)}) collective-permute-start(bf16[256,1024]{1,0:T(8,128)(2,1)} %get-tuple-element.46.refs_18_), channel_id=1, source_target_pairs={{0,4},{4,0},{8,12},{12,8},{16,20},{20,16},{24,28},{28,24},{1,5},{5... | collective-permute-start | bytes 1572872 | tf_op jit(solution)/shard_map/ppermute | solution.py:38
  51.6 7.9 %collective-permute-start.20 = (bf16[256,1024]{1,0:T(8,128)(2,1)}, bf16[256,1024]{1,0:T(8,128)(2,1)S(1)}, u32[]{:S(2)}, u32[]{:S(2)}) collective-permute-start(bf16[256,1024]{1,0:T(8,128)(2,1)} %collective-permute-done.18.refs_21_), channel_id=1, source_target_pairs={{0,4},{4,0},{8,12},{12,8},{16,20},{20,16},{24,28},{28,24},{1,5},{5... | collective-permute-start | bytes 1572872 | tf_op jit(solution)/shard_map/ppermute | solution.py:38
  52.0 7.6 %collective-permute-start.25 = (bf16[256,1024]{1,0:T(8,128)(2,1)}, bf16[256,1024]{1,0:T(8,128)(2,1)S(1)}, u32[]{:S(2)}, u32[]{:S(2)}) collective-permute-start(bf16[256,1024]{1,0:T(8,128)(2,1)} %collective-permute-done.23.refs_26_), channel_id=1, source_target_pairs={{0,4},{4,0},{8,12},{12,8},{16,20},{20,16},{24,28},{28,24},{1,5},{5... | collective-permute-start | bytes 1572872 | tf_op jit(solution)/shard_map/ppermute | solution.py:38
  52.1 9.0 %collective-permute-start.21 = (bf16[256,1024]{1,0:T(8,128)(2,1)}, bf16[256,1024]{1,0:T(8,128)(2,1)S(1)}, u32[]{:S(2)}, u32[]{:S(2)}) collective-permute-start(bf16[256,1024]{1,0:T(8,128)(2,1)} %collective-permute-done.19.refs_22_), channel_id=1, source_target_pairs={{0,4},{4,0},{8,12},{12,8},{16,20},{20,16},{24,28},{28,24},{1,5},{5... | collective-permute-start | bytes 1572872 | tf_op jit(solution)/shard_map/ppermute | solution.py:38
  54.7 99.8 %copy-start.6 = (bf16[3,256,512]{2,1,0:T(8,128)(2,1)}, bf16[3,256,512]{2,1,0:T(8,128)(2,1)S(1)}, u32[]{:S(2)}) copy-start(bf16[3,256,512]{2,1,0:T(8,128)(2,1)S(1)} %pad_maximum_fusion.1.refs_6_) | copy-start | bytes 2359300
  55.6 37.7 %collective-permute-start.30 = (bf16[256,1024]{1,0:T(8,128)(2,1)}, bf16[256,1024]{1,0:T(8,128)(2,1)S(1)}, u32[]{:S(2)}, u32[]{:S(2)}) collective-permute-start(bf16[256,1024]{1,0:T(8,128)(2,1)} %collective-permute-done.18.refs_21_), channel_id=1, source_target_pairs={{0,16},{4,20},{8,24},{12,28},{16,0},{20,4},{24,8},{28,12},{1,17},{... | collective-permute-start | bytes 1572872 | tf_op jit(solution)/shard_map/ppermute | solution.py:38
  58.0 39.7 %collective-permute-start.31 = (bf16[256,1024]{1,0:T(8,128)(2,1)}, bf16[256,1024]{1,0:T(8,128)(2,1)}, u32[]{:S(2)}, u32[]{:S(2)}) collective-permute-start(bf16[256,1024]{1,0:T(8,128)(2,1)} %collective-permute-done.23.refs_26_), channel_id=1, source_target_pairs={{0,8},{4,12},{8,0},{12,4},{16,24},{20,28},{24,16},{28,20},{1,9},{5... | collective-permute-start | bytes 1572872 | tf_op jit(solution)/shard_map/ppermute | solution.py:38
  59.5 33.8 %collective-permute-start.24 = (bf16[256,1024]{1,0:T(8,128)(2,1)}, bf16[256,1024]{1,0:T(8,128)(2,1)}, u32[]{:S(2)}, u32[]{:S(2)}) collective-permute-start(bf16[256,1024]{1,0:T(8,128)(2,1)} %collective-permute-done.22.refs_25_), channel_id=1, source_target_pairs={{0,4},{4,0},{8,12},{12,8},{16,20},{20,16},{24,28},{28,24},{1,5},{5... | collective-permute-start | bytes 1572872 | tf_op jit(solution)/shard_map/ppermute | solution.py:38
  60.6 55.6 %collective-permute-start.13 = (bf16[3,256,512]{2,1,0:T(8,128)(2,1)S(1)}, bf16[3,256,512]{2,1,0:T(8,128)(2,1)}, u32[]{:S(2)}, u32[]{:S(2)}) collective-permute-start(bf16[3,256,512]{2,1,0:T(8,128)(2,1)S(1)} %pad_maximum_fusion.1.refs_6_), channel_id=1, source_target_pairs={{0,16},{4,20},{8,24},{12,28},{16,0},{20,4},{24,8},{28,12},{1,17},{... | collective-permute-start | bytes 2359304 | tf_op jit(solution)/shard_map/ppermute | solution.py:38
  61.9 54.8 %collective-permute-start.8 = (bf16[3,256,512]{2,1,0:T(8,128)(2,1)S(1)}, bf16[3,256,512]{2,1,0:T(8,128)(2,1)}, u32[]{:S(2)}, u32[]{:S(2)}) collective-permute-start(bf16[3,256,512]{2,1,0:T(8,128)(2,1)S(1)} %pad_maximum_fusion.refs_5_), channel_id=1, source_target_pairs={{0,8},{4,12},{8,0},{12,4},{16,24},{20,28},{24,16},{28,20},{1,9},{5... | collective-permute-start | bytes 2359304 | tf_op jit(solution)/shard_map/ppermute | solution.py:38
  93.3 11.1 %collective-permute-start = (bf16[8,128,128]{2,1,0:T(8,128)(2,1)S(1)}, bf16[8,128,128]{2,1,0:T(8,128)(2,1)S(1)}, u32[]{:S(2)}, u32[]{:S(2)}) collective-permute-start(bf16[8,128,128]{2,1,0:T(8,128)(2,1)S(1)} %all_to_all.10.refs_0_), channel_id=1, source_target_pairs={{0,1},{1,2},{2,3},{3,0},{4,5},{5,6},{6,7},{7,4},{8,9},{9,10},{10,1... | collective-permute-start | bytes 786440 | tf_op jit(solution)/shard_map/ppermute | solution.py:43
  93.3 20.9 %collective-permute-start.1 = (bf16[8,128,128]{2,1,0:T(8,128)(2,1)S(1)}, bf16[8,128,128]{2,1,0:T(8,128)(2,1)S(1)}, u32[]{:S(2)}, u32[]{:S(2)}) collective-permute-start(bf16[8,128,128]{2,1,0:T(8,128)(2,1)S(1)} %all_to_all.10.refs_0_), channel_id=1, source_target_pairs={{0,2},{1,3},{2,0},{3,1},{4,6},{5,7},{6,4},{7,5},{8,10},{9,11},{10,... | collective-permute-start | bytes 786440 | tf_op jit(solution)/shard_map/ppermute | solution.py:43
  97.7 17.8 %collective-permute-start.2 = (bf16[8,128,128]{2,1,0:T(8,128)(2,1)S(1)}, bf16[8,128,128]{2,1,0:T(8,128)(2,1)S(1)}, u32[]{:S(2)}, u32[]{:S(2)}) collective-permute-start(bf16[8,128,128]{2,1,0:T(8,128)(2,1)S(1)} %all_to_all.10.refs_0_), channel_id=1, source_target_pairs={{0,3},{1,0},{2,1},{3,2},{4,7},{5,4},{6,5},{7,6},{8,11},{9,8},{10,9... | collective-permute-start | bytes 786440 | tf_op jit(solution)/shard_map/ppermute | solution.py:43
  105.1 17.1 %collective-permute-start.9 = (bf16[3,256,512]{2,1,0:T(8,128)(2,1)S(1)}, bf16[3,256,512]{2,1,0:T(8,128)(2,1)}, u32[]{:S(2)}, u32[]{:S(2)}) collective-permute-start(bf16[3,256,512]{2,1,0:T(8,128)(2,1)S(1)} %pad_maximum_fusion.1.refs_6_), channel_id=1, source_target_pairs={{0,8},{4,12},{8,0},{12,4},{16,24},{20,28},{24,16},{28,20},{1,9},{5... | collective-permute-start | bytes 2359304 | tf_op jit(solution)/shard_map/ppermute | solution.py:38
  115.0 19.5 %collective-permute-start.12 = (bf16[3,256,512]{2,1,0:T(8,128)(2,1)S(1)}, bf16[3,256,512]{2,1,0:T(8,128)(2,1)}, u32[]{:S(2)}, u32[]{:S(2)}) collective-permute-start(bf16[3,256,512]{2,1,0:T(8,128)(2,1)S(1)} %pad_maximum_fusion.refs_5_), channel_id=1, source_target_pairs={{0,16},{4,20},{8,24},{12,28},{16,0},{20,4},{24,8},{28,12},{1,17},{... | collective-permute-start | bytes 2359304 | tf_op jit(solution)/shard_map/ppermute | solution.py:38
  116.2 18.8 %collective-permute-start.7 = (bf16[3,256,512]{2,1,0:T(8,128)(2,1)S(1)}, bf16[3,256,512]{2,1,0:T(8,128)(2,1)S(1)}, u32[]{:S(2)}, u32[]{:S(2)}) collective-permute-start(bf16[3,256,512]{2,1,0:T(8,128)(2,1)S(1)} %pad_maximum_fusion.1.refs_6_), channel_id=1, source_target_pairs={{0,4},{4,0},{8,12},{12,8},{16,20},{20,16},{24,28},{28,24},{1,5},{5... | collective-permute-start | bytes 2359304 | tf_op jit(solution)/shard_map/ppermute | solution.py:38
  116.2 19.7 %collective-permute-start.6 = (bf16[3,256,512]{2,1,0:T(8,128)(2,1)S(1)}, bf16[3,256,512]{2,1,0:T(8,128)(2,1)S(1)}, u32[]{:S(2)}, u32[]{:S(2)}) collective-permute-start(bf16[3,256,512]{2,1,0:T(8,128)(2,1)S(1)} %pad_maximum_fusion.refs_5_), channel_id=1, source_target_pairs={{0,4},{4,0},{8,12},{12,8},{16,20},{20,16},{24,28},{28,24},{1,5},{5... | collective-permute-start | bytes 2359304 | tf_op jit(solution)/shard_map/ppermute | solution.py:38
  116.7 20.5 %collective-permute-start.15 = (bf16[3,256,512]{2,1,0:T(8,128)(2,1)}, bf16[3,256,512]{2,1,0:T(8,128)(2,1)S(1)}, u32[]{:S(2)}, u32[]{:S(2)}) collective-permute-start(bf16[3,256,512]{2,1,0:T(8,128)(2,1)} %collective-permute-done.13.refs_14_), channel_id=1, source_target_pairs={{0,4},{4,0},{8,12},{12,8},{16,20},{20,16},{24,28},{28,24},{1,5},{5... | collective-permute-start | bytes 2359304 | tf_op jit(solution)/shard_map/ppermute | solution.py:38
  122.2 21.2 %collective-permute-start.27 = (bf16[3,256,512]{2,1,0:T(8,128)(2,1)}, bf16[3,256,512]{2,1,0:T(8,128)(2,1)S(1)}, u32[]{:S(2)}, u32[]{:S(2)}) collective-permute-start(bf16[3,256,512]{2,1,0:T(8,128)(2,1)} %collective-permute-done.13.refs_14_), channel_id=1, source_target_pairs={{0,8},{4,12},{8,0},{12,4},{16,24},{20,28},{24,16},{28,20},{1,9},{5... | collective-permute-start | bytes 2359304 | tf_op jit(solution)/shard_map/ppermute | solution.py:38
  134.4 18.8 %collective-permute-start.26 = (bf16[3,256,512]{2,1,0:T(8,128)(2,1)}, bf16[3,256,512]{2,1,0:T(8,128)(2,1)}, u32[]{:S(2)}, u32[]{:S(2)}) collective-permute-start(bf16[3,256,512]{2,1,0:T(8,128)(2,1)} %collective-permute-done.8.refs_9_), channel_id=1, source_target_pairs={{0,16},{4,20},{8,24},{12,28},{16,0},{20,4},{24,8},{28,12},{1,17},{... | collective-permute-start | bytes 2359304 | tf_op jit(solution)/shard_map/ppermute | solution.py:38
  135.9 18.8 %collective-permute-start.10 = (bf16[3,256,512]{2,1,0:T(8,128)(2,1)}, bf16[3,256,512]{2,1,0:T(8,128)(2,1)}, u32[]{:S(2)}, u32[]{:S(2)}) collective-permute-start(bf16[3,256,512]{2,1,0:T(8,128)(2,1)} %collective-permute-done.8.refs_9_), channel_id=1, source_target_pairs={{0,4},{4,0},{8,12},{12,8},{16,20},{20,16},{24,28},{28,24},{1,5},{5... | collective-permute-start | bytes 2359304 | tf_op jit(solution)/shard_map/ppermute | solution.py:38
  136.7 18.5 %collective-permute-start.11 = (bf16[3,256,512]{2,1,0:T(8,128)(2,1)}, bf16[3,256,512]{2,1,0:T(8,128)(2,1)}, u32[]{:S(2)}, u32[]{:S(2)}) collective-permute-start(bf16[3,256,512]{2,1,0:T(8,128)(2,1)} %collective-permute-done.9.refs_10_), channel_id=1, source_target_pairs={{0,4},{4,0},{8,12},{12,8},{16,20},{20,16},{24,28},{28,24},{1,5},{5... | collective-permute-start | bytes 2359304 | tf_op jit(solution)/shard_map/ppermute | solution.py:38
  138.2 17.1 %collective-permute-start.14 = (bf16[3,256,512]{2,1,0:T(8,128)(2,1)}, bf16[3,256,512]{2,1,0:T(8,128)(2,1)}, u32[]{:S(2)}, u32[]{:S(2)}) collective-permute-start(bf16[3,256,512]{2,1,0:T(8,128)(2,1)} %collective-permute-done.12.refs_13_), channel_id=1, source_target_pairs={{0,4},{4,0},{8,12},{12,8},{16,20},{20,16},{24,28},{28,24},{1,5},{5... | collective-permute-start | bytes 2359304 | tf_op jit(solution)/shard_map/ppermute | solution.py:38
  143.4 36.1 %collective-permute-start.29 = (bf16[3,256,512]{2,1,0:T(8,128)(2,1)S(1)}, bf16[3,256,512]{2,1,0:T(8,128)(2,1)}, u32[]{:S(2)}, u32[]{:S(2)}) collective-permute-start(bf16[3,256,512]{2,1,0:T(8,128)(2,1)S(1)} %collective-permute-done.27.refs_5_), channel_id=1, source_target_pairs={{0,4},{4,0},{8,12},{12,8},{16,20},{20,16},{24,28},{28,24},{1,5},{5... | collective-permute-start | bytes 2359304 | tf_op jit(solution)/shard_map/ppermute | solution.py:38
  153.3 26.3 %collective-permute-start.28 = (bf16[3,256,512]{2,1,0:T(8,128)(2,1)}, bf16[3,256,512]{2,1,0:T(8,128)(2,1)}, u32[]{:S(2)}, u32[]{:S(2)}) collective-permute-start(bf16[3,256,512]{2,1,0:T(8,128)(2,1)} %collective-permute-done.26.refs_4_), channel_id=1, source_target_pairs={{0,4},{4,0},{8,12},{12,8},{16,20},{20,16},{24,28},{28,24},{1,5},{5... | collective-permute-start | bytes 2359304 | tf_op jit(solution)/shard_map/ppermute | solution.py:38
  154.6 24.9 %collective-permute-start.32 = (bf16[256,1024]{1,0:T(8,128)(2,1)S(1)}, bf16[256,1024]{1,0:T(8,128)(2,1)}, u32[]{:S(2)}, u32[]{:S(2)}) collective-permute-start(bf16[256,1024]{1,0:T(8,128)(2,1)S(1)} %collective-permute-done.30.refs_8_), channel_id=1, source_target_pairs={{0,4},{4,0},{8,12},{12,8},{16,20},{20,16},{24,28},{28,24},{1,5},{5... | collective-permute-start | bytes 1572872 | tf_op jit(solution)/shard_map/ppermute | solution.py:38
  155.2 24.3 %collective-permute-start.33 = (bf16[256,1024]{1,0:T(8,128)(2,1)}, bf16[256,1024]{1,0:T(8,128)(2,1)}, u32[]{:S(2)}, u32[]{:S(2)}) collective-permute-start(bf16[256,1024]{1,0:T(8,128)(2,1)} %collective-permute-done.31.refs_9_), channel_id=1, source_target_pairs={{0,4},{4,0},{8,12},{12,8},{16,20},{20,16},{24,28},{28,24},{1,5},{5... | collective-permute-start | bytes 1572872 | tf_op jit(solution)/shard_map/ppermute | solution.py:38
  191.0 9.8 %collective-permute-start.40 = (bf16[64,1536]{1,0:T(8,128)(2,1)S(1)}, bf16[64,1536]{1,0:T(8,128)(2,1)S(1)}, u32[]{:S(2)}, u32[]{:S(2)}) collective-permute-start(bf16[64,1536]{1,0:T(8,128)(2,1)S(1)} %get-tuple-element.37), channel_id=1, source_target_pairs={{0,1},{1,2},{2,3},{3,0},{4,5},{5,6},{6,7},{7,4},{8,9},{9,10},{10,1... | collective-permute-start | bytes 589832 | tf_op jit(solution)/shard_map/ppermute | solution.py:43
  191.0 17.6 %collective-permute-start.41 = (bf16[64,1536]{1,0:T(8,128)(2,1)S(1)}, bf16[64,1536]{1,0:T(8,128)(2,1)S(1)}, u32[]{:S(2)}, u32[]{:S(2)}) collective-permute-start(bf16[64,1536]{1,0:T(8,128)(2,1)S(1)} %get-tuple-element.38), channel_id=1, source_target_pairs={{0,2},{1,3},{2,0},{3,1},{4,6},{5,7},{6,4},{7,5},{8,10},{9,11},{10,... | collective-permute-start | bytes 589832 | tf_op jit(solution)/shard_map/ppermute | solution.py:43
  193.3 15.3 %collective-permute-start.42 = (bf16[64,1536]{1,0:T(8,128)(2,1)S(1)}, bf16[64,1536]{1,0:T(8,128)(2,1)S(1)}, u32[]{:S(2)}, u32[]{:S(2)}) collective-permute-start(bf16[64,1536]{1,0:T(8,128)(2,1)S(1)} %get-tuple-element.39), channel_id=1, source_target_pairs={{0,3},{1,0},{2,1},{3,2},{4,7},{5,4},{6,5},{7,6},{8,11},{9,8},{10,9... | collective-permute-start | bytes 589832 | tf_op jit(solution)/shard_map/ppermute | solution.py:43
  194.8 29.1 %collective-permute-start.34 = (bf16[64,1536]{1,0:T(8,128)(2,1)S(1)}, bf16[64,1536]{1,0:T(8,128)(2,1)S(1)}, u32[]{:S(2)}, u32[]{:S(2)}) collective-permute-start(bf16[64,1536]{1,0:T(8,128)(2,1)S(1)} %get-tuple-element.28), channel_id=1, source_target_pairs={{0,1},{1,2},{2,3},{3,0},{4,5},{5,6},{6,7},{7,4},{8,9},{9,10},{10,1... | collective-permute-start | bytes 589832 | tf_op jit(solution)/shard_map/ppermute | solution.py:43
  195.4 31.8 %collective-permute-start.35 = (bf16[64,1536]{1,0:T(8,128)(2,1)S(1)}, bf16[64,1536]{1,0:T(8,128)(2,1)S(1)}, u32[]{:S(2)}, u32[]{:S(2)}) collective-permute-start(bf16[64,1536]{1,0:T(8,128)(2,1)S(1)} %get-tuple-element.29), channel_id=1, source_target_pairs={{0,2},{1,3},{2,0},{3,1},{4,6},{5,7},{6,4},{7,5},{8,10},{9,11},{10,... | collective-permute-start | bytes 589832 | tf_op jit(solution)/shard_map/ppermute | solution.py:43
  200.7 26.5 %collective-permute-start.36 = (bf16[64,1536]{1,0:T(8,128)(2,1)S(1)}, bf16[64,1536]{1,0:T(8,128)(2,1)S(1)}, u32[]{:S(2)}, u32[]{:S(2)}) collective-permute-start(bf16[64,1536]{1,0:T(8,128)(2,1)S(1)} %get-tuple-element.30), channel_id=1, source_target_pairs={{0,3},{1,0},{2,1},{3,2},{4,7},{5,4},{6,5},{7,6},{8,11},{9,8},{10,9... | collective-permute-start | bytes 589832 | tf_op jit(solution)/shard_map/ppermute | solution.py:43
  210.8 24.8 %collective-permute-start.43 = (bf16[64,512]{1,0:T(8,128)(2,1)S(1)}, bf16[64,512]{1,0:T(8,128)(2,1)S(1)}, u32[]{:S(2)}, u32[]{:S(2)}) collective-permute-start(bf16[64,512]{1,0:T(8,128)(2,1)S(1)} %get-tuple-element.41), channel_id=1, source_target_pairs={{0,1},{1,2},{2,3},{3,0},{4,5},{5,6},{6,7},{7,4},{8,9},{9,10},{10,1... | collective-permute-start | bytes 196616 | tf_op jit(solution)/shard_map/ppermute | solution.py:43
  223.9 14.1 %collective-permute-start.44 = (bf16[64,512]{1,0:T(8,128)(2,1)S(1)}, bf16[64,512]{1,0:T(8,128)(2,1)S(1)}, u32[]{:S(2)}, u32[]{:S(2)}) collective-permute-start(bf16[64,512]{1,0:T(8,128)(2,1)S(1)} %get-tuple-element.42), channel_id=1, source_target_pairs={{0,2},{1,3},{2,0},{3,1},{4,6},{5,7},{6,4},{7,5},{8,10},{9,11},{10,... | collective-permute-start | bytes 196616 | tf_op jit(solution)/shard_map/ppermute | solution.py:43
  224.0 14.0 %collective-permute-start.45 = (bf16[64,512]{1,0:T(8,128)(2,1)S(1)}, bf16[64,512]{1,0:T(8,128)(2,1)S(1)}, u32[]{:S(2)}, u32[]{:S(2)}) collective-permute-start(bf16[64,512]{1,0:T(8,128)(2,1)S(1)} %get-tuple-element.43), channel_id=1, source_target_pairs={{0,3},{1,0},{2,1},{3,2},{4,7},{5,4},{6,5},{7,6},{8,11},{9,8},{10,9... | collective-permute-start | bytes 196616 | tf_op jit(solution)/shard_map/ppermute | solution.py:43
  229.3 8.7 %collective-permute-start.37 = (bf16[64,512]{1,0:T(8,128)(2,1)S(1)}, bf16[64,512]{1,0:T(8,128)(2,1)S(1)}, u32[]{:S(2)}, u32[]{:S(2)}) collective-permute-start(bf16[64,512]{1,0:T(8,128)(2,1)S(1)} %get-tuple-element.32), channel_id=1, source_target_pairs={{0,1},{1,2},{2,3},{3,0},{4,5},{5,6},{6,7},{7,4},{8,9},{9,10},{10,1... | collective-permute-start | bytes 196616 | tf_op jit(solution)/shard_map/ppermute | solution.py:43
  235.6 5.4 %collective-permute-start.38 = (bf16[64,512]{1,0:T(8,128)(2,1)S(1)}, bf16[64,512]{1,0:T(8,128)(2,1)S(1)}, u32[]{:S(2)}, u32[]{:S(2)}) collective-permute-start(bf16[64,512]{1,0:T(8,128)(2,1)S(1)} %get-tuple-element.33), channel_id=1, source_target_pairs={{0,2},{1,3},{2,0},{3,1},{4,6},{5,7},{6,4},{7,5},{8,10},{9,11},{10,... | collective-permute-start | bytes 196616 | tf_op jit(solution)/shard_map/ppermute | solution.py:43
  235.6 5.4 %collective-permute-start.39 = (bf16[64,512]{1,0:T(8,128)(2,1)S(1)}, bf16[64,512]{1,0:T(8,128)(2,1)S(1)}, u32[]{:S(2)}, u32[]{:S(2)}) collective-permute-start(bf16[64,512]{1,0:T(8,128)(2,1)S(1)} %get-tuple-element.34), channel_id=1, source_target_pairs={{0,3},{1,0},{2,1},{3,2},{4,7},{5,4},{6,5},{7,6},{8,11},{9,8},{10,9... | collective-permute-start | bytes 196616 | tf_op jit(solution)/shard_map/ppermute | solution.py:43
  (38 other events, 430.8 us)

commit v2 on v1

--- a/solution.py
+++ b/solution.py
@@ -15,15 +15,16 @@
 F32 = jnp.float32
 BF16 = jnp.bfloat16
 CHUNKS = 2
-VMEM_LIMIT = 32 * 1024 * 1024
-EARLY_LIMIT = 40 * 1024 * 1024
-LATE_LIMIT = 32 * 1024 * 1024
+MIB = 1024 * 1024
 
 
 VM = pl.BlockSpec(memory_space=pltpu.VMEM)
 SM = pl.BlockSpec(memory_space=pltpu.SMEM)
 ANY = pl.BlockSpec(memory_space=pl.ANY)
-PARAMS = pltpu.CompilerParams(vmem_limit_bytes=VMEM_LIMIT)
+
+
+def limit(mib):
+    return pltpu.CompilerParams(vmem_limit_bytes=mib * MIB)
 
 
 def cost(flops, moved):
@@ -47,19 +48,28 @@
     return [1 << place for place in range(1, size.bit_length() - 1)]
 
 
-def spread(piece, axis, order):
+def spread(piece, axis, order, trim):
     held = {0: piece}
+    far = sum(order)
     for bit in order:
-        held.update({at ^ bit: flip(v, axis, bit) for at, v in list(held.items())})
+        found = {}
+        for at, value in held.items():
+            to = at ^ bit
+            found[to] = flip(trim(value) if to == far else value, axis, bit)
+        held.update(found)
     held.update({at ^ 1: flip(v, axis, 1) for at, v in list(held.items())})
     return held
 
 
-def spread_halves(first, second, axis):
+def spread_halves(first, second, axis, trim=lambda value: value):
     size = lax.axis_size(axis)
-    a = spread(first, axis, ici_bits(size))
-    b = spread(second, axis, ici_bits(size)[::-1])
+    a = spread(first, axis, ici_bits(size), trim)
+    b = spread(second, axis, ici_bits(size)[::-1], trim)
     return [half for at in range(size) for half in (a[at], b[at])]
+
+
+def direct_steps(books):
+    return [1, books - 1] if books > 3 else []
 
 
 def project_body(hidden_ref, gain_ref, weight_ref, out_ref, normed_ref):
@@ -102,7 +112,7 @@
         out_specs=pl.BlockSpec((seqs, per, frames, HD), lambda i: (0, i % parts, 0, i // parts)),
         out_shape=jax.ShapeDtypeStruct((seqs, heads, frames, 3 * HD), BF16),
         scratch_shapes=[pltpu.VMEM((rows, width), BF16)],
-        compiler_params=PARAMS,
+        compiler_params=limit(58),
         cost_estimate=cost(6 * rows * width * cols, 6 * width * cols + 2 * rows * width),
     )(hidden.reshape(rows, width), gain.reshape(1, width), weight)
 
@@ -138,7 +148,7 @@
         in_specs=[VM],
         out_specs=VM,
         out_shape=jax.ShapeDtypeStruct((length, HD), BF16),
-        compiler_params=PARAMS,
+        compiler_params=limit(20),
         cost_estimate=cost(3 * length * length * HD, 8 * length * HD),
     )(packed)
 
@@ -274,7 +284,7 @@
             pltpu.SemaphoreType.DMA((2 * count, 4)),
             pltpu.SemaphoreType.DMA((count, 4)),
         ],
-        compiler_params=pltpu.CompilerParams(vmem_limit_bytes=EARLY_LIMIT),
+        compiler_params=limit(30),
         cost_estimate=cost(
             2 * rows * width * (groups * cols + deep), 2 * width * (groups * cols + deep)
         ),
@@ -288,18 +298,21 @@
     )
 
 
-def put_qkv(normed, weights, out_refs, full_ref, book):
+def put_qkv(normed, weights, part, out_refs, full_ref, book):
     books = len(out_refs)
     block, wide = out_refs[0].shape
     cols = wide // 3
     for which in range(3):
-        full_ref[:, which * cols : (which + 1) * cols] = dot(normed, weights[which])
+        weight = weights[which, :, part * cols : (part + 1) * cols]
+        full_ref[:, which * cols : (which + 1) * cols] = dot(normed, weight)
     for at in range(books):
         row = pl.multiple_of(lax.rem(book + at, books) * block, block)
         out_refs[at][...] = full_ref[pl.ds(row, block), :].astype(BF16)
 
 
-def late_output(place, early, acc, hidden, mixed, own, out_pieces, in_pieces, entry, gain, weights, late, chunks):
+def late_output(
+    place, early, acc, hidden, mixed, own, out_pieces, direct, in_pieces, entry, gain, weights, late, chunks
+):
     rows, width = hidden.shape
     books = len(mixed)
     size = len(out_pieces) // 2
@@ -309,51 +322,82 @@
     part = deep // chunks
     share = rows // books
     used = [2 * (late + core) + side for core in range(2) for side in range(2)]
+    steps = sorted(direct)
+    first = 2 if steps else 1
+    count = out_pieces[used[0]].shape[0]
+    fars = [direct[step][core].reshape(2, cols // 2, block) for core in range(2) for step in steps]
 
     def body(place_ref, _, acc_ref, hidden_ref, entry_ref, gain_ref, own_ref, qkv_ref, *refs):
-        mixed_refs = refs[:books]
-        outs = refs[books : books + 4]
-        ins = refs[books + 4 : books + 8]
-        out_ref, stream_ref, normed_ref = refs[books + 8 : books + 11]
-        out_refs = refs[books + 11 : 2 * books + 11]
-        cat_ref, own_buf, qkv_buf, full_ref, late_buf, sems = refs[2 * books + 11 :]
+        mixed_refs, refs = refs[:books], refs[books:]
+        ins, refs = refs[:4], refs[4:]
+        outs, refs = refs[:4], refs[4:]
+        far_refs, refs = refs[: len(fars)], refs[len(fars) :]
+        out_ref, stream_ref, normed_ref = refs[:3]
+        out_refs = refs[3 : 3 + books]
+        cat_ref, out_buf, full_ref, old_buf, new_buf, sems, ends = refs[3 + books :]
         me = place_ref[0]
         book = place_ref[1]
         start = chip_start(me, late, 2 * block)
-        fetch_own = pltpu.make_async_copy(own_ref.at[:, pl.ds(start, 2 * block)], own_buf, sems.at[0])
-        fetch_qkv = pltpu.make_async_copy(qkv_ref.at[:, :, 0:part], qkv_buf, sems.at[1])
-        fetch_own.start()
-        fetch_qkv.start()
+
+        def copies(core):
+            column = pl.multiple_of((me ^ (late + core)) * block, block)
+            found = []
+            for side in range(2):
+                found.append(
+                    pltpu.make_async_copy(
+                        own_ref.at[side * (cols // 2) : (side + 1) * (cols // 2), pl.ds(column, block)],
+                        out_buf.at[core, 0, side],
+                        sems.at[core, side],
+                    )
+                )
+                found.append(
+                    pltpu.make_async_copy(
+                        outs[2 * core + side],
+                        out_buf.at[core, first : first + count, side],
+                        sems.at[core, 2 + side],
+                    )
+                )
+            for index, step in enumerate(steps):
+                found.append(
+                    pltpu.make_async_copy(
+                        far_refs[core * len(steps) + index],
+                        out_buf.at[core, step],
+                        sems.at[core, 4 + index],
+                    )
+                )
+            return found
+
+        old = pltpu.make_async_copy(hidden_ref.at[:, pl.ds(start, 2 * block)], old_buf, ends.at[0])
+        for core in range(2):
+            for copy in copies(core):
+                copy.start()
+        old.start()
         put_mixed(mixed_refs, cat_ref)
-        fetch_own.wait()
         total = acc_ref[...] + entry_ref[...].astype(F32)
         for core in range(2):
-            column = pl.multiple_of((me ^ (late + core)) * block, block)
-            span = pl.ds(column, block)
             local = pl.ds(pl.multiple_of(((me ^ core) & 1) * block, block), block)
-            summed = dot(cat_ref[:, :cols], own_buf[:, local])
-            for side in range(2):
-                for group in range(1, books):
-                    at = group * cols + side * (cols // 2)
-                    summed += dot(cat_ref[:, at : at + cols // 2], outs[2 * core + side][group - 1])
-            value = (hidden_ref[:, span].astype(F32) + summed).astype(BF16)
-            late_buf[:, local] = value
+            for copy in copies(core):
+                copy.wait()
+            if core == 0:
+                old.wait()
+            summed = dot(cat_ref[...], out_buf[core].reshape(books * cols, block))
+            value = (old_buf[:, local].astype(F32) + summed).astype(BF16)
+            new_buf[:, local] = value
             for side in range(2):
                 total += dot(value[:, side * half : (side + 1) * half], ins[2 * core + side][...])
-        put = pltpu.make_async_copy(late_buf, out_ref.at[:, pl.ds(start, 2 * block)], sems.at[2])
+        put = pltpu.make_async_copy(new_buf, out_ref.at[:, pl.ds(start, 2 * block)], ends.at[1])
         put.start()
         stream = total.astype(BF16)
         stream_ref[...] = stream
         values = stream.astype(F32)
         mean_sq = jnp.mean(values * values, axis=-1, keepdims=True)
         normed_ref[...] = (values * lax.rsqrt(mean_sq + EPS) * gain_ref[...]).astype(BF16)
-        fetch_qkv.wait()
-        put_qkv(normed_ref[...], qkv_buf, out_refs, full_ref, book)
+        put_qkv(normed_ref[...], qkv_ref, 0, out_refs, full_ref, book)
         put.wait()
 
     return pl.pallas_call(
         body,
-        in_specs=[SM, ANY, VM, VM, VM, VM, ANY, ANY] + [VM] * (books + 8),
+        in_specs=[SM, ANY, VM, ANY, VM, VM, ANY, VM] + [VM] * (books + 4) + [ANY] * (4 + len(fars)),
         out_specs=[ANY] + [VM] * (2 + books),
         out_shape=[jax.ShapeDtypeStruct((rows, width), BF16)]
         + [jax.ShapeDtypeStruct((rows, deep), BF16)] * 2
@@ -361,13 +405,14 @@
         input_output_aliases={1: 0},
         scratch_shapes=[
             pltpu.VMEM((rows, books * cols), BF16),
-            pltpu.VMEM((cols, 2 * block), BF16),
-            pltpu.VMEM((3, deep, part), BF16),
+            pltpu.VMEM((2, books, 2, cols // 2, block), BF16),
             pltpu.VMEM((rows, 3 * part), F32),
             pltpu.VMEM((rows, 2 * block), BF16),
-            pltpu.SemaphoreType.DMA((3,)),
+            pltpu.VMEM((rows, 2 * block), BF16),
+            pltpu.SemaphoreType.DMA((2, 4 + len(steps))),
+            pltpu.SemaphoreType.DMA((2,)),
         ],
-        compiler_params=pltpu.CompilerParams(vmem_limit_bytes=LATE_LIMIT),
+        compiler_params=limit(20),
         cost_estimate=cost(
             rows * width * (books * cols + deep) // 2 + 6 * rows * deep * part,
             width * (books * cols + deep) // 2 + 6 * deep * part,
@@ -382,8 +427,9 @@
         own,
         weights,
         *mixed,
+        *[in_pieces[i] for i in used],
         *[out_pieces[i] for i in used],
-        *[in_pieces[i] for i in used],
+        *fars,
     )
 
 
@@ -393,20 +439,15 @@
     block = rows // books
 
     def body(place_ref, normed_ref, qkv_ref, *refs):
-        put_qkv(normed_ref[...], qkv_ref, refs[:books], refs[books], place_ref[1])
+        put_qkv(normed_ref[...], qkv_ref, part, refs[:books], refs[books], place_ref[1])
 
     return pl.pallas_call(
         body,
-        grid=(1,),
-        in_specs=[
-            SM,
-            pl.BlockSpec((rows, deep), lambda i: (0, 0)),
-            pl.BlockSpec((3, deep, cols), lambda i: (0, 0, part)),
-        ],
-        out_specs=[pl.BlockSpec((block, 3 * cols), lambda i: (0, 0))] * books,
+        in_specs=[SM, VM, VM],
+        out_specs=[VM] * books,
         out_shape=[jax.ShapeDtypeStruct((block, 3 * cols), BF16)] * books,
         scratch_shapes=[pltpu.VMEM((rows, 3 * cols), F32)],
-        compiler_params=PARAMS,
+        compiler_params=limit(20),
         cost_estimate=cost(6 * rows * deep * cols, 6 * deep * cols),
     )(place, normed, weights)
 
@@ -459,7 +500,7 @@
         out_specs=[VM] * books,
         out_shape=[jax.ShapeDtypeStruct((rows, cols), BF16)] * books,
         scratch_shapes=[pltpu.VMEM((books, rows, wide), BF16), pltpu.VMEM((books, rows, cols), BF16)],
-        compiler_params=PARAMS,
+        compiler_params=limit(20),
         cost_estimate=cost(4 * books * books * rows * cols * 128, 8 * books * rows * cols),
     )(place, *arrived)
 
@@ -489,7 +530,7 @@
         out_specs=VM,
         out_shape=jax.ShapeDtypeStruct((rows, deep), BF16),
         scratch_shapes=[pltpu.VMEM((rows, deep), BF16)],
-        compiler_params=PARAMS,
+        compiler_params=limit(20),
         cost_estimate=cost(2 * rows * deep * deep, 2 * deep * deep),
     )(place, stream, weight, *flat)
 
@@ -523,18 +564,25 @@
     half = cols // 2
     first = jnp.stack([piece[:half] for piece in ring[1:]])
     second = jnp.stack([piece[half:] for piece in ring[1:]])
-    out_pieces = spread_halves(first, second, "seq")
+    steps = direct_steps(books)
+    trim = (lambda value: value[1:-1]) if steps else (lambda value: value)
+    out_pieces = spread_halves(first, second, "seq", trim)
+    late = size - 2
+    there = lax.dynamic_slice_in_dim(temporal_out, (lax.axis_index("seq") ^ late) * block, block, 1)
+    direct = {}
+    for step in steps:
+        piece = shift(there, "cb", step)
+        direct[step] = (piece, flip(piece, "seq", 1))
 
     entry = jnp.take(embedding[0], codebook_ids.reshape(rows), axis=0)
 
     packed = project(hidden, temporal_gain, temporal_qkv)
     own_mixed = temporal_attention(packed)
     mixed = [own_mixed] + [shift(own_mixed, "cb", by) for by in range(1, books)]
-    late = size - 2
     flat = hidden.reshape(rows, width)
     early, acc = early_output(place, flat, mixed, temporal_out, out_pieces, in_pieces, late)
     temporal, stream, normed, *sent = late_output(
-        place, early, acc, flat, mixed, temporal_out, out_pieces, in_pieces,
+        place, early, acc, flat, mixed, temporal_out, out_pieces, direct, in_pieces,
         entry, depth_gain, depth_qkv[0], late, CHUNKS,
     )
     arrived, returned = [], []

time: 244 us -> 250 us (1.025)
  blocking collectives: 28.6 us -> 17.2 us
  starting transfers between devices: 58.2 us -> 65.7 us
  local copies, waits for them, and re-layouts: 42.7 us -> 46.1 us
  waiting for transfers between devices: 77.8 us -> 80.7 us
    all_to_all x1, blocking collectives: 28.6 us -> 17.2 us  [temporal_attention(): lax.all_to_all(mixed.reshape(size, frames, HD), 'seq', split_axis=0, conc...]
    ppermute x28 -> x30, waiting for transfers between devices: 25.3 us -> 33.2 us  [flip(): lax.ppermute(x, axis, [(i, i ^ bit) for i in range(lax.axis_size(axis))])]
    ppermute x18 -> x20, waiting for transfers between devices: 51.9 us -> 47.6 us  [shift(): return lax.ppermute(x, axis, [(i, (i + by) % size) for i in range(size)])]
    ppermute x18 -> x20, starting transfers between devices: 39.4 us -> 43.5 us  [shift(): return lax.ppermute(x, axis, [(i, (i + by) % size) for i in range(size)])]
    pallas_call x1, Pallas kernels: 7.06 us -> 10.5 us  [project(): pl.pallas_call(project_body, grid=(3 * parts,), in_specs=[pl.BlockSpec((r...]
    slice x0 -> x2, local copies, waits for them, and re-layouts: none -> 3.39 us  [shards(): trim = (lambda value: value[1:-1]) if steps else lambda value: value]
    ppermute x28 -> x30, starting transfers between devices: 15.3 us -> 18.5 us  [flip(): lax.ppermute(x, axis, [(i, i ^ bit) for i in range(lax.axis_size(axis))])]
    unnamed x78 -> x90, local copies, waits for them, and re-layouts: 30.9 us -> 28.8 us
  transfers between devices with their start and end apart: 47 -> 51, of which waited for: 12 -> 16; matrix products, arithmetic and copies ran while one was open for 5% -> 7% of each run, Pallas kernels for 10% -> 10%
where the time goes in v2:
time: 250 us; the launch traced here: 249 us
  waiting for transfers between devices  80.7 us (32%)
  starting transfers between devices  65.7 us (26%)
  local copies, waits for them, and re-layouts  46.1 us (18%)
  Pallas kernels  35.2 us (14%)
  blocking collectives  17.2 us (7%)
  other arithmetic  2.83 us (1%)
    ppermute x20, waiting for transfers between devices, shift(): return lax.ppermute(x, axis, [(i, (i + by) % size) for i in range(size)])  47.6 us
    ppermute x20, starting transfers between devices, shift(): return lax.ppermute(x, axis, [(i, (i + by) % size) for i in range(size)])  43.5 us
    ppermute x30, waiting for transfers between devices, flip(): lax.ppermute(x, axis, [(i, i ^ bit) for i in range(lax.axis_size(axis))])  33.2 us
    unnamed x90, local copies, waits for them, and re-layouts  28.8 us
    ppermute x30, starting transfers between devices, flip(): lax.ppermute(x, axis, [(i, i ^ bit) for i in range(lax.axis_size(axis))])  18.5 us
    all_to_all x1, blocking collectives, temporal_attention(): lax.all_to_all(mixed.reshape(size, frames, HD), 'seq', split_axis=0, conc...  17.2 us
    pallas_call x1, Pallas kernels, project(): pl.pallas_call(project_body, grid=(3 * parts,), in_specs=[pl.BlockSpec((r...  10.5 us
    pallas_call x1, Pallas kernels, early_output(): pl.pallas_call(body, in_specs=[SM, VM] + [VM] * groups + [ANY] * (1 + 8 *...  9 us
  transfers between devices with their start and end apart: 51, of which 16 were waited for; matrix products, arithmetic and copies ran while one was open for 7% of the time, Pallas kernels for 10%

profile of v2, /device:TPU:0, one launch (start us, length us, event | category | flops | bytes accessed | tf_op | source)
XLA Modules:
  0.0 248.6 jit_solution(615867865583772180)
XLA Ops:
  0.6 2.1 constant_dynamic-slice_fusion
  2.7 3.1 %collective-permute-start.3 = (bf16[512,512]{1,0:T(8,128)(2,1)S(1)}, bf16[512,512]{1,0:T(8,128)(2,1)S(1)}, u32[]{:S(2)}, u32[]{:S(2)}) collective-permute-start(bf16[512,512]{1,0:T(8,128)(2,1)S(1)} %get-tuple-element.47), channel_id=1, source_target_pairs={{0,1},{1,2},{2,3},{3,0},{4,5},{5,6},{6,7},{7,4},{8,9},{9,10},{10,1... | collective-permute-start | bytes 1572872 | tf_op jit(solution)/shard_map/ppermute | solution.py:44
  7.0 1.6 collective-permute-start.18
  8.6 1.5 collective-permute-start.23
  11.2 8.5 %collective-permute-done.3 = bf16[512,512]{1,0:T(8,128)(2,1)S(1)} collective-permute-done((bf16[512,512]{1,0:T(8,128)(2,1)S(1)}, bf16[512,512]{1,0:T(8,128)(2,1)S(1)}, u32[]{:S(2)}, u32[]{:S(2)}) %collective-permute-start.3) | collective-permute-done | bytes 524320 | tf_op jit(solution)/shard_map/ppermute | solution.py:44
  22.0 1.6 collective-permute-start.4
  23.6 8.2 %collective-permute-done.19.refs_22_ = bf16[256,1024]{1,0:T(8,128)(2,1)} collective-permute-done((bf16[256,1024]{1,0:T(8,128)(2,1)S(1)}, bf16[256,1024]{1,0:T(8,128)(2,1)}, u32[]{:S(2)}, u32[]{:S(2)}) %collective-permute-start.19) | collective-permute-done | bytes 524320 | tf_op jit(solution)/shard_map/ppermute | solution.py:39
  31.8 1.6 collective-permute-start.34
  33.4 2.2 collective-permute-start.35
  36.5 2.0 collective-permute-done.4
  38.5 10.5 %shard_map.113 = bf16[2,4,128,384]{3,2,1,0:T(8,128)(2,1)} custom-call(bf16[256,4096]{1,0:T(8,128)(2,1)} %bitcast.42, f32[1,4096]{1,0:T(1,128)} %bitcast.56, bf16[3,4096,512]{2,1,0:T(8,128)(2,1)} %weight_ref.1), custom_call_target="tpu_custom_call" | custom-call | flops 3221225472 | bytes 14680064 | tf_op jit(solution)/shard_map/pallas_call | solution.py:104
  49.0 3.7 %all-to-all-start = ((bf16[8,128,384]{2,1,0:T(8,128)(2,1)}), bf16[8,128,384]{2,1,0:T(8,128)(2,1)S(1)}, u32[]{:S(2)}, u32[]{:S(2)}) async-start(bf16[8,128,384]{2,1,0:T(8,128)(2,1)} %bitcast.53), calls=%async_computation | async-start | bytes 1572864 | tf_op jit(solution)/shard_map/all_to_all | solution.py:161
  52.7 1.8 slice_bitcast_fusion.4
  55.1 1.9 slice_bitcast_fusion.3
  57.0 3.7 %collective-permute-done.35 = bf16[512,512]{1,0:T(8,128)(2,1)S(1)} collective-permute-done((bf16[512,512]{1,0:T(8,128)(2,1)}, bf16[512,512]{1,0:T(8,128)(2,1)S(1)}, u32[]{:S(2)}, u32[]{:S(2)}) %collective-permute-start.35) | collective-permute-done | bytes 524320 | tf_op jit(solution)/shard_map/ppermute | solution.py:44
  60.7 1.5 collective-permute-start.26
  63.0 7.6 %collective-permute-done.5 = bf16[512,512]{1,0:T(8,128)(2,1)} collective-permute-done((bf16[512,512]{1,0:T(8,128)(2,1)}, bf16[512,512]{1,0:T(8,128)(2,1)}, u32[]{:S(2)}, u32[]{:S(2)}) %collective-permute-start.5) | collective-permute-done | bytes 524320 | tf_op jit(solution)/shard_map/ppermute | solution.py:44
  70.5 1.8 slice_bitcast_fusion.2
  77.1 1.8 shard_map.114
  78.9 17.2 %all_to_all.10.refs_0_ = bf16[8,128,128]{2,1,0:T(8,128)(2,1)S(1)} all-to-all(bf16[8,128,128]{2,1,0:T(8,128)(2,1)S(1)} %bitcast.51), channel_id=1, replica_groups=mesh['seq'=8,'cb'=4] {'seq'}, dimensions={0} | all-to-all | bytes 524288 | tf_op jit(solution)/shard_map/all_to_all | solution.py:163
  96.9 3.6 %collective-permute-start.1 = (bf16[8,128,128]{2,1,0:T(8,128)(2,1)S(1)}, bf16[8,128,128]{2,1,0:T(8,128)(2,1)S(1)}, u32[]{:S(2)}, u32[]{:S(2)}) collective-permute-start(bf16[8,128,128]{2,1,0:T(8,128)(2,1)S(1)} %all_to_all.10.refs_0_), channel_id=1, source_target_pairs={{0,2},{1,3},{2,0},{3,1},{4,6},{5,7},{6,4},{7,5},{8,10},{9,11},{10,... | collective-permute-start | bytes 786440 | tf_op jit(solution)/shard_map/ppermute | solution.py:44
  102.6 1.5 collective-permute-start.8
  104.1 3.0 %collective-permute-done.refs_1_ = bf16[8,128,128]{2,1,0:T(8,128)(2,1)S(1)} collective-permute-done((bf16[8,128,128]{2,1,0:T(8,128)(2,1)S(1)}, bf16[8,128,128]{2,1,0:T(8,128)(2,1)S(1)}, u32[]{:S(2)}, u32[]{:S(2)}) %collective-permute-start) | collective-permute-done | bytes 262176 | tf_op jit(solution)/shard_map/ppermute | solution.py:44
  109.3 7.6 %collective-permute-done.1.refs_2_ = bf16[8,128,128]{2,1,0:T(8,128)(2,1)S(1)} collective-permute-done((bf16[8,128,128]{2,1,0:T(8,128)(2,1)S(1)}, bf16[8,128,128]{2,1,0:T(8,128)(2,1)S(1)}, u32[]{:S(2)}, u32[]{:S(2)}) %collective-permute-start.1) | collective-permute-done | bytes 262176 | tf_op jit(solution)/shard_map/ppermute | solution.py:44
  117.6 1.5 collective-permute-start.12
  121.2 2.0 collective-permute-done.8.refs_9_
  123.2 15.1 %collective-permute-done.9.refs_10_ = bf16[3,256,512]{2,1,0:T(8,128)(2,1)} collective-permute-done((bf16[3,256,512]{2,1,0:T(8,128)(2,1)S(1)}, bf16[3,256,512]{2,1,0:T(8,128)(2,1)}, u32[]{:S(2)}, u32[]{:S(2)}) %collective-permute-start.9) | collective-permute-done | bytes 786464 | tf_op jit(solution)/shard_map/ppermute | solution.py:39
  139.8 1.7 slice.49
  142.5 1.7 collective-permute-start.31
  144.2 1.7 slice.48
  145.9 5.6 %collective-permute-done.31.refs_9_ = bf16[1,256,512]{2,1,0:T(8,128)(2,1)} collective-permute-done((bf16[1,256,512]{2,1,0:T(8,128)(2,1)}, bf16[1,256,512]{2,1,0:T(8,128)(2,1)}, u32[]{:S(2)}, u32[]{:S(2)}) %collective-permute-start.31) | collective-permute-done | bytes 262176 | tf_op jit(solution)/shard_map/ppermute | solution.py:39
  152.5 5.1 %gather_fusion = bf16[256,1024]{1,0:T(8,128)(2,1)} fusion(bf16[2048,1024]{1,0:T(8,128)(2,1)} %bitcast.52, s32[1024]{0:T(1024)S(1)} %pad_clamp_fusion), kind=kCustom, calls=%fused_computation | custom fusion | bytes 1049600 | tf_op jit(solution)/shard_map/jit(_take)/gather | solution.py:577
  160.8 2.2 copy-done.1
  175.6 9.0 %shard_map.115 = (bf16[256,4096]{1,0:T(8,128)(2,1)}, f32[256,1024]{1,0:T(8,128)S(1)}) custom-call(s32[2]{0:T(128)S(1)} %pad_add_fusion.place_ref, bf16[256,4096]{1,0:T(8,128)(2,1)S(1)} %bitcast.43, bf16[8,128,128]{2,1,0:T(8,128)(2,1)S(1)} %all_to_all.10.refs_0_, bf16[8,128,128]{2,1,0:T(8,128)(2,1)S(1)} %copy-done.19, bf16[8,128,128]{2,1,0:T(8,128)(2,1)S(1)} %copy-done.21, ...), custom_call_target="tpu_custom_call" | custom-call | flops 6442450944 | bytes 25165824 | tf_op jit(solution)/shard_map/pallas_call | solution.py:272
  185.4 2.2 copy-done.2
  188.5 6.0 %shard_map.116 = (bf16[256,4096]{1,0:T(8,128)(2,1)}, bf16[256,1024]{1,0:T(8,128)(2,1)S(1)}, bf16[256,1024]{1,0:T(8,128)(2,1)S(1)}, bf16[64,1536]{1,0:T(8,128)(2,...) custom-call(s32[2]{0:T(128)S(1)} %pad_add_fusion.place_ref, ...), custom_call_target="tpu_custom_call", output_to_operand_aliasing={{0}: (1, {})} | custom-call | flops 2415919104 | bytes 9437184 | tf_op jit(solution)/shard_map/pallas_call | solution.py:398
  194.5 1.7 shard_map.118
  197.2 1.8 collective-permute-start.45
  202.2 3.8 %collective-permute-done.44.refs_1_ = bf16[64,1536]{1,0:T(8,128)(2,1)S(1)} collective-permute-done((bf16[64,1536]{1,0:T(8,128)(2,1)S(1)}, bf16[64,1536]{1,0:T(8,128)(2,1)S(1)}, u32[]{:S(2)}, u32[]{:S(2)}) %collective-permute-start.44) | collective-permute-done | bytes 196640 | tf_op jit(solution)/shard_map/ppermute | solution.py:44
  207.3 7.2 %collective-permute-done.45.refs_2_ = bf16[64,1536]{1,0:T(8,128)(2,1)S(1)} collective-permute-done((bf16[64,1536]{1,0:T(8,128)(2,1)S(1)}, bf16[64,1536]{1,0:T(8,128)(2,1)S(1)}, u32[]{:S(2)}, u32[]{:S(2)}) %collective-permute-start.45) | collective-permute-done | bytes 196640 | tf_op jit(solution)/shard_map/ppermute | solution.py:44
  214.5 2.1 shard_map.119
  216.6 13.3 %collective-permute-start.47 = (bf16[64,512]{1,0:T(8,128)(2,1)S(1)}, bf16[64,512]{1,0:T(8,128)(2,1)S(1)}, u32[]{:S(2)}, u32[]{:S(2)}) collective-permute-start(bf16[64,512]{1,0:T(8,128)(2,1)S(1)} %get-tuple-element.41), channel_id=1, source_target_pairs={{0,1},{1,2},{2,3},{3,0},{4,5},{5,6},{6,7},{7,4},{8,9},{9,10},{10,1... | collective-permute-start | bytes 196616 | tf_op jit(solution)/shard_map/ppermute | solution.py:44
  229.8 2.4 collective-permute-start.49
  232.9 2.1 shard_map.117
  235.0 5.5 %collective-permute-start.41 = (bf16[64,512]{1,0:T(8,128)(2,1)S(1)}, bf16[64,512]{1,0:T(8,128)(2,1)S(1)}, u32[]{:S(2)}, u32[]{:S(2)}) collective-permute-start(bf16[64,512]{1,0:T(8,128)(2,1)S(1)} %get-tuple-element.32), channel_id=1, source_target_pairs={{0,1},{1,2},{2,3},{3,0},{4,5},{5,6},{6,7},{7,4},{8,9},{9,10},{10,1... | collective-permute-start | bytes 196616 | tf_op jit(solution)/shard_map/ppermute | solution.py:44
  240.5 2.4 collective-permute-start.43
  243.0 3.5 %collective-permute-done.42.refs_2_ = bf16[64,512]{1,0:T(8,128)(2,1)S(1)} collective-permute-done((bf16[64,512]{1,0:T(8,128)(2,1)S(1)}, bf16[64,512]{1,0:T(8,128)(2,1)S(1)}, u32[]{:S(2)}, u32[]{:S(2)}) %collective-permute-start.42) | collective-permute-done | bytes 65568 | tf_op jit(solution)/shard_map/ppermute | solution.py:44
  246.5 2.1 shard_map.120
  (169 shorter events, 46.6 us)
Async XLA Ops:
  2.7 17.0 %collective-permute-start.3 = (bf16[512,512]{1,0:T(8,128)(2,1)S(1)}, bf16[512,512]{1,0:T(8,128)(2,1)S(1)}, u32[]{:S(2)}, u32[]{:S(2)}) collective-permute-start(bf16[512,512]{1,0:T(8,128)(2,1)S(1)} %get-tuple-element.47), channel_id=1, source_target_pairs={{0,1},{1,2},{2,3},{3,0},{4,5},{5,6},{6,7},{7,4},{8,9},{9,10},{10,1... | collective-permute-start | bytes 1572872 | tf_op jit(solution)/shard_map/ppermute | solution.py:44
  7.0 15.0 %collective-permute-start.18 = (bf16[256,1024]{1,0:T(8,128)(2,1)S(1)}, bf16[256,1024]{1,0:T(8,128)(2,1)}, u32[]{:S(2)}, u32[]{:S(2)}) collective-permute-start(bf16[256,1024]{1,0:T(8,128)(2,1)S(1)} %get-tuple-element.49.refs_17_), channel_id=1, source_target_pairs={{0,8},{4,12},{8,0},{12,4},{16,24},{20,28},{24,16},{28,20},{1,9},{5... | collective-permute-start | bytes 1572872 | tf_op jit(solution)/shard_map/ppermute | solution.py:39
  8.6 15.0 %collective-permute-start.23 = (bf16[256,1024]{1,0:T(8,128)(2,1)S(1)}, bf16[256,1024]{1,0:T(8,128)(2,1)}, u32[]{:S(2)}, u32[]{:S(2)}) collective-permute-start(bf16[256,1024]{1,0:T(8,128)(2,1)S(1)} %get-tuple-element.48.refs_18_), channel_id=1, source_target_pairs={{0,16},{4,20},{8,24},{12,28},{16,0},{20,4},{24,8},{28,12},{1,17},{... | collective-permute-start | bytes 1572872 | tf_op jit(solution)/shard_map/ppermute | solution.py:39
  10.1 21.7 %collective-permute-start.19 = (bf16[256,1024]{1,0:T(8,128)(2,1)S(1)}, bf16[256,1024]{1,0:T(8,128)(2,1)}, u32[]{:S(2)}, u32[]{:S(2)}) collective-permute-start(bf16[256,1024]{1,0:T(8,128)(2,1)S(1)} %get-tuple-element.48.refs_18_), channel_id=1, source_target_pairs={{0,8},{4,12},{8,0},{12,4},{16,24},{20,28},{24,16},{28,20},{1,9},{5... | collective-permute-start | bytes 1572872 | tf_op jit(solution)/shard_map/ppermute | solution.py:39
  10.7 22.8 %collective-permute-start.22 = (bf16[256,1024]{1,0:T(8,128)(2,1)S(1)}, bf16[256,1024]{1,0:T(8,128)(2,1)}, u32[]{:S(2)}, u32[]{:S(2)}) collective-permute-start(bf16[256,1024]{1,0:T(8,128)(2,1)S(1)} %get-tuple-element.49.refs_17_), channel_id=1, source_target_pairs={{0,16},{4,20},{8,24},{12,28},{16,0},{20,4},{24,8},{28,12},{1,17},{... | collective-permute-start | bytes 1572872 | tf_op jit(solution)/shard_map/ppermute | solution.py:39
  19.7 16.0 %collective-permute-start.16 = (bf16[256,1024]{1,0:T(8,128)(2,1)S(1)}, bf16[256,1024]{1,0:T(8,128)(2,1)S(1)}, u32[]{:S(2)}, u32[]{:S(2)}) collective-permute-start(bf16[256,1024]{1,0:T(8,128)(2,1)S(1)} %get-tuple-element.49.refs_17_), channel_id=1, source_target_pairs={{0,4},{4,0},{8,12},{12,8},{16,20},{20,16},{24,28},{28,24},{1,5},{5... | collective-permute-start | bytes 1572872 | tf_op jit(solution)/shard_map/ppermute | solution.py:39
  22.0 16.4 %collective-permute-start.4 = (bf16[512,512]{1,0:T(8,128)(2,1)S(1)}, bf16[512,512]{1,0:T(8,128)(2,1)}, u32[]{:S(2)}, u32[]{:S(2)}) collective-permute-start(bf16[512,512]{1,0:T(8,128)(2,1)S(1)} %collective-permute-done.3), channel_id=1, source_target_pairs={{0,1},{1,2},{2,3},{3,0},{4,5},{5,6},{6,7},{7,4},{8,9},{9,10},{10,1... | collective-permute-start | bytes 1572872 | tf_op jit(solution)/shard_map/ppermute | solution.py:44
  23.6 30.9 %collective-permute-start.17 = (bf16[256,1024]{1,0:T(8,128)(2,1)S(1)}, bf16[256,1024]{1,0:T(8,128)(2,1)S(1)}, u32[]{:S(2)}, u32[]{:S(2)}) collective-permute-start(bf16[256,1024]{1,0:T(8,128)(2,1)S(1)} %get-tuple-element.48.refs_18_), channel_id=1, source_target_pairs={{0,4},{4,0},{8,12},{12,8},{16,20},{20,16},{24,28},{28,24},{1,5},{5... | collective-permute-start | bytes 1572872 | tf_op jit(solution)/shard_map/ppermute | solution.py:39
  31.8 23.2 %collective-permute-start.34 = (bf16[512,512]{1,0:T(8,128)(2,1)}, bf16[512,512]{1,0:T(8,128)(2,1)S(1)}, u32[]{:S(2)}, u32[]{:S(2)}) collective-permute-start(bf16[512,512]{1,0:T(8,128)(2,1)} %get-tuple-element.46), channel_id=1, source_target_pairs={{0,1},{1,2},{2,3},{3,0},{4,5},{5,6},{6,7},{7,4},{8,9},{9,10},{10,1... | collective-permute-start | bytes 1572872 | tf_op jit(solution)/shard_map/ppermute | solution.py:44
  33.4 27.3 %collective-permute-start.35 = (bf16[512,512]{1,0:T(8,128)(2,1)}, bf16[512,512]{1,0:T(8,128)(2,1)S(1)}, u32[]{:S(2)}, u32[]{:S(2)}) collective-permute-start(bf16[512,512]{1,0:T(8,128)(2,1)} %get-tuple-element.46), channel_id=1, source_target_pairs={{0,3},{1,0},{2,1},{3,2},{4,7},{5,4},{6,5},{7,6},{8,11},{9,8},{10,9... | collective-permute-start | bytes 1572872 | tf_op jit(solution)/shard_map/ppermute | solution.py:44
  36.5 25.7 %collective-permute-start.20 = (bf16[256,1024]{1,0:T(8,128)(2,1)}, bf16[256,1024]{1,0:T(8,128)(2,1)S(1)}, u32[]{:S(2)}, u32[]{:S(2)}) collective-permute-start(bf16[256,1024]{1,0:T(8,128)(2,1)} %collective-permute-done.18.refs_21_), channel_id=1, source_target_pairs={{0,4},{4,0},{8,12},{12,8},{16,20},{20,16},{24,28},{28,24},{1,5},{5... | collective-permute-start | bytes 1572872 | tf_op jit(solution)/shard_map/ppermute | solution.py:39
  38.4 32.1 %collective-permute-start.5 = (bf16[512,512]{1,0:T(8,128)(2,1)}, bf16[512,512]{1,0:T(8,128)(2,1)}, u32[]{:S(2)}, u32[]{:S(2)}) collective-permute-start(bf16[512,512]{1,0:T(8,128)(2,1)} %collective-permute-done.4), channel_id=1, source_target_pairs={{0,1},{1,2},{2,3},{3,0},{4,5},{5,6},{6,7},{7,4},{8,9},{9,10},{10,1... | collective-permute-start | bytes 1572872 | tf_op jit(solution)/shard_map/ppermute | solution.py:44
  49.0 28.1 %all-to-all-start = ((bf16[8,128,384]{2,1,0:T(8,128)(2,1)}), bf16[8,128,384]{2,1,0:T(8,128)(2,1)S(1)}, u32[]{:S(2)}, u32[]{:S(2)}) async-start(bf16[8,128,384]{2,1,0:T(8,128)(2,1)} %bitcast.53), calls=%async_computation | async-start | bytes 1572864 | tf_op jit(solution)/shard_map/all_to_all | solution.py:161
  54.5 17.9 %collective-permute-start.25 = (bf16[256,1024]{1,0:T(8,128)(2,1)}, bf16[256,1024]{1,0:T(8,128)(2,1)S(1)}, u32[]{:S(2)}, u32[]{:S(2)}) collective-permute-start(bf16[256,1024]{1,0:T(8,128)(2,1)} %collective-permute-done.23.refs_26_), channel_id=1, source_target_pairs={{0,4},{4,0},{8,12},{12,8},{16,20},{20,16},{24,28},{28,24},{1,5},{5... | collective-permute-start | bytes 1572872 | tf_op jit(solution)/shard_map/ppermute | solution.py:39
  55.0 19.8 %collective-permute-start.21 = (bf16[256,1024]{1,0:T(8,128)(2,1)}, bf16[256,1024]{1,0:T(8,128)(2,1)S(1)}, u32[]{:S(2)}, u32[]{:S(2)}) collective-permute-start(bf16[256,1024]{1,0:T(8,128)(2,1)} %collective-permute-done.19.refs_22_), channel_id=1, source_target_pairs={{0,4},{4,0},{8,12},{12,8},{16,20},{20,16},{24,28},{28,24},{1,5},{5... | collective-permute-start | bytes 1572872 | tf_op jit(solution)/shard_map/ppermute | solution.py:39
  60.7 39.8 %collective-permute-start.26 = (bf16[256,1024]{1,0:T(8,128)(2,1)}, bf16[256,1024]{1,0:T(8,128)(2,1)S(1)}, u32[]{:S(2)}, u32[]{:S(2)}) collective-permute-start(bf16[256,1024]{1,0:T(8,128)(2,1)} %collective-permute-done.18.refs_21_), channel_id=1, source_target_pairs={{0,16},{4,20},{8,24},{12,28},{16,0},{20,4},{24,8},{28,12},{1,17},{... | collective-permute-start | bytes 1572872 | tf_op jit(solution)/shard_map/ppermute | solution.py:39
  63.0 33.0 %collective-permute-start.24 = (bf16[256,1024]{1,0:T(8,128)(2,1)}, bf16[256,1024]{1,0:T(8,128)(2,1)}, u32[]{:S(2)}, u32[]{:S(2)}) collective-permute-start(bf16[256,1024]{1,0:T(8,128)(2,1)} %collective-permute-done.22.refs_25_), channel_id=1, source_target_pairs={{0,4},{4,0},{8,12},{12,8},{16,20},{20,16},{24,28},{28,24},{1,5},{5... | collective-permute-start | bytes 1572872 | tf_op jit(solution)/shard_map/ppermute | solution.py:39
  70.5 25.5 %collective-permute-start.36 = (bf16[512,512]{1,0:T(8,128)(2,1)S(1)}, bf16[512,512]{1,0:T(8,128)(2,1)S(1)}, u32[]{:S(2)}, u32[]{:S(2)}) collective-permute-start(bf16[512,512]{1,0:T(8,128)(2,1)S(1)} %collective-permute-done.34), channel_id=1, source_target_pairs={{0,4},{4,0},{8,12},{12,8},{16,20},{20,16},{24,28},{28,24},{1,5},{5... | collective-permute-start | bytes 1572872 | tf_op jit(solution)/shard_map/ppermute | solution.py:39
  73.3 46.5 %collective-permute-start.13 = (bf16[3,256,512]{2,1,0:T(8,128)(2,1)S(1)}, bf16[3,256,512]{2,1,0:T(8,128)(2,1)}, u32[]{:S(2)}, u32[]{:S(2)}) collective-permute-start(bf16[3,256,512]{2,1,0:T(8,128)(2,1)S(1)} %pad_maximum_fusion.1.refs_6_), channel_id=1, source_target_pairs={{0,16},{4,20},{8,24},{12,28},{16,0},{20,4},{24,8},{28,12},{1,17},{... | collective-permute-start | bytes 2359304 | tf_op jit(solution)/shard_map/ppermute | solution.py:39
  75.6 27.0 %collective-permute-start.27 = (bf16[256,1024]{1,0:T(8,128)(2,1)}, bf16[256,1024]{1,0:T(8,128)(2,1)}, u32[]{:S(2)}, u32[]{:S(2)}) collective-permute-start(bf16[256,1024]{1,0:T(8,128)(2,1)} %collective-permute-done.23.refs_26_), channel_id=1, source_target_pairs={{0,8},{4,12},{8,0},{12,4},{16,24},{20,28},{24,16},{28,20},{1,9},{5... | collective-permute-start | bytes 1572872 | tf_op jit(solution)/shard_map/ppermute | solution.py:39
  96.0 11.1 %collective-permute-start = (bf16[8,128,128]{2,1,0:T(8,128)(2,1)S(1)}, bf16[8,128,128]{2,1,0:T(8,128)(2,1)S(1)}, u32[]{:S(2)}, u32[]{:S(2)}) collective-permute-start(bf16[8,128,128]{2,1,0:T(8,128)(2,1)S(1)} %all_to_all.10.refs_0_), channel_id=1, source_target_pairs={{0,1},{1,2},{2,3},{3,0},{4,5},{5,6},{6,7},{7,4},{8,9},{9,10},{10,1... | collective-permute-start | bytes 786440 | tf_op jit(solution)/shard_map/ppermute | solution.py:44
  96.9 20.0 %collective-permute-start.1 = (bf16[8,128,128]{2,1,0:T(8,128)(2,1)S(1)}, bf16[8,128,128]{2,1,0:T(8,128)(2,1)S(1)}, u32[]{:S(2)}, u32[]{:S(2)}) collective-permute-start(bf16[8,128,128]{2,1,0:T(8,128)(2,1)S(1)} %all_to_all.10.refs_0_), channel_id=1, source_target_pairs={{0,2},{1,3},{2,0},{3,1},{4,6},{5,7},{6,4},{7,5},{8,10},{9,11},{10,... | collective-permute-start | bytes 786440 | tf_op jit(solution)/shard_map/ppermute | solution.py:44
  100.5 18.6 %collective-permute-start.2 = (bf16[8,128,128]{2,1,0:T(8,128)(2,1)S(1)}, bf16[8,128,128]{2,1,0:T(8,128)(2,1)S(1)}, u32[]{:S(2)}, u32[]{:S(2)}) collective-permute-start(bf16[8,128,128]{2,1,0:T(8,128)(2,1)S(1)} %all_to_all.10.refs_0_), channel_id=1, source_target_pairs={{0,3},{1,0},{2,1},{3,2},{4,7},{5,4},{6,5},{7,6},{8,11},{9,8},{10,9... | collective-permute-start | bytes 786440 | tf_op jit(solution)/shard_map/ppermute | solution.py:44
  102.6 20.6 %collective-permute-start.8 = (bf16[3,256,512]{2,1,0:T(8,128)(2,1)S(1)}, bf16[3,256,512]{2,1,0:T(8,128)(2,1)}, u32[]{:S(2)}, u32[]{:S(2)}) collective-permute-start(bf16[3,256,512]{2,1,0:T(8,128)(2,1)S(1)} %pad_maximum_fusion.refs_5_), channel_id=1, source_target_pairs={{0,8},{4,12},{8,0},{12,4},{16,24},{20,28},{24,16},{28,20},{1,9},{5... | collective-permute-start | bytes 2359304 | tf_op jit(solution)/shard_map/ppermute | solution.py:39
  107.9 30.4 %collective-permute-start.9 = (bf16[3,256,512]{2,1,0:T(8,128)(2,1)S(1)}, bf16[3,256,512]{2,1,0:T(8,128)(2,1)}, u32[]{:S(2)}, u32[]{:S(2)}) collective-permute-start(bf16[3,256,512]{2,1,0:T(8,128)(2,1)S(1)} %pad_maximum_fusion.1.refs_6_), channel_id=1, source_target_pairs={{0,8},{4,12},{8,0},{12,4},{16,24},{20,28},{24,16},{28,20},{1,9},{5... | collective-permute-start | bytes 2359304 | tf_op jit(solution)/shard_map/ppermute | solution.py:39
  117.6 20.7 %collective-permute-start.12 = (bf16[3,256,512]{2,1,0:T(8,128)(2,1)S(1)}, bf16[3,256,512]{2,1,0:T(8,128)(2,1)}, u32[]{:S(2)}, u32[]{:S(2)}) collective-permute-start(bf16[3,256,512]{2,1,0:T(8,128)(2,1)S(1)} %pad_maximum_fusion.refs_5_), channel_id=1, source_target_pairs={{0,16},{4,20},{8,24},{12,28},{16,0},{20,4},{24,8},{28,12},{1,17},{... | collective-permute-start | bytes 2359304 | tf_op jit(solution)/shard_map/ppermute | solution.py:39
  119.8 19.0 %collective-permute-start.7 = (bf16[3,256,512]{2,1,0:T(8,128)(2,1)S(1)}, bf16[3,256,512]{2,1,0:T(8,128)(2,1)S(1)}, u32[]{:S(2)}, u32[]{:S(2)}) collective-permute-start(bf16[3,256,512]{2,1,0:T(8,128)(2,1)S(1)} %pad_maximum_fusion.1.refs_6_), channel_id=1, source_target_pairs={{0,4},{4,0},{8,12},{12,8},{16,20},{20,16},{24,28},{28,24},{1,5},{5... | collective-permute-start | bytes 2359304 | tf_op jit(solution)/shard_map/ppermute | solution.py:39
  119.8 21.7 %collective-permute-start.6 = (bf16[3,256,512]{2,1,0:T(8,128)(2,1)S(1)}, bf16[3,256,512]{2,1,0:T(8,128)(2,1)S(1)}, u32[]{:S(2)}, u32[]{:S(2)}) collective-permute-start(bf16[3,256,512]{2,1,0:T(8,128)(2,1)S(1)} %pad_maximum_fusion.refs_5_), channel_id=1, source_target_pairs={{0,4},{4,0},{8,12},{12,8},{16,20},{20,16},{24,28},{28,24},{1,5},{5... | collective-permute-start | bytes 2359304 | tf_op jit(solution)/shard_map/ppermute | solution.py:39
  123.2 36.5 %collective-permute-start.15 = (bf16[3,256,512]{2,1,0:T(8,128)(2,1)}, bf16[3,256,512]{2,1,0:T(8,128)(2,1)}, u32[]{:S(2)}, u32[]{:S(2)}) collective-permute-start(bf16[3,256,512]{2,1,0:T(8,128)(2,1)} %collective-permute-done.13.refs_14_), channel_id=1, source_target_pairs={{0,4},{4,0},{8,12},{12,8},{16,20},{20,16},{24,28},{28,24},{1,5},{5... | collective-permute-start | bytes 2359304 | tf_op jit(solution)/shard_map/ppermute | solution.py:39
  138.3 21.9 %collective-permute-start.10 = (bf16[3,256,512]{2,1,0:T(8,128)(2,1)}, bf16[3,256,512]{2,1,0:T(8,128)(2,1)}, u32[]{:S(2)}, u32[]{:S(2)}) collective-permute-start(bf16[3,256,512]{2,1,0:T(8,128)(2,1)} %collective-permute-done.8.refs_9_), channel_id=1, source_target_pairs={{0,4},{4,0},{8,12},{12,8},{16,20},{20,16},{24,28},{28,24},{1,5},{5... | collective-permute-start | bytes 2359304 | tf_op jit(solution)/shard_map/ppermute | solution.py:39
  138.3 22.0 %collective-permute-start.11 = (bf16[3,256,512]{2,1,0:T(8,128)(2,1)}, bf16[3,256,512]{2,1,0:T(8,128)(2,1)}, u32[]{:S(2)}, u32[]{:S(2)}) collective-permute-start(bf16[3,256,512]{2,1,0:T(8,128)(2,1)} %collective-permute-done.9.refs_10_), channel_id=1, source_target_pairs={{0,4},{4,0},{8,12},{12,8},{16,20},{20,16},{24,28},{28,24},{1,5},{5... | collective-permute-start | bytes 2359304 | tf_op jit(solution)/shard_map/ppermute | solution.py:39
  139.8 20.9 %collective-permute-start.14 = (bf16[3,256,512]{2,1,0:T(8,128)(2,1)}, bf16[3,256,512]{2,1,0:T(8,128)(2,1)}, u32[]{:S(2)}, u32[]{:S(2)}) collective-permute-start(bf16[3,256,512]{2,1,0:T(8,128)(2,1)} %collective-permute-done.12.refs_13_), channel_id=1, source_target_pairs={{0,4},{4,0},{8,12},{12,8},{16,20},{20,16},{24,28},{28,24},{1,5},{5... | collective-permute-start | bytes 2359304 | tf_op jit(solution)/shard_map/ppermute | solution.py:39
  142.5 9.0 %collective-permute-start.31 = (bf16[1,256,512]{2,1,0:T(8,128)(2,1)}, bf16[1,256,512]{2,1,0:T(8,128)(2,1)}, u32[]{:S(2)}, u32[]{:S(2)}) collective-permute-start(bf16[1,256,512]{2,1,0:T(8,128)(2,1)} %slice.49), channel_id=1, source_target_pairs={{0,8},{4,12},{8,0},{12,4},{16,24},{20,28},{24,16},{28,20},{1,9},{5... | collective-permute-start | bytes 786440 | tf_op jit(solution)/shard_map/ppermute | solution.py:39
  151.5 8.2 %collective-permute-start.30 = (bf16[1,256,512]{2,1,0:T(8,128)(2,1)}, bf16[1,256,512]{2,1,0:T(8,128)(2,1)}, u32[]{:S(2)}, u32[]{:S(2)}) collective-permute-start(bf16[1,256,512]{2,1,0:T(8,128)(2,1)} %slice.48), channel_id=1, source_target_pairs={{0,16},{4,20},{8,24},{12,28},{16,0},{20,4},{24,8},{28,12},{1,17},{... | collective-permute-start | bytes 786440 | tf_op jit(solution)/shard_map/ppermute | solution.py:39
  159.7 24.9 %collective-permute-start.37 = (bf16[512,512]{1,0:T(8,128)(2,1)}, bf16[512,512]{1,0:T(8,128)(2,1)S(1)}, u32[]{:S(2)}, u32[]{:S(2)}) collective-permute-start(bf16[512,512]{1,0:T(8,128)(2,1)} %copy-done.8), channel_id=1, source_target_pairs={{0,4},{4,0},{8,12},{12,8},{16,20},{20,16},{24,28},{28,24},{1,5},{5... | collective-permute-start | bytes 1572872 | tf_op jit(solution)/shard_map/ppermute | solution.py:39
  159.7 24.9 %collective-permute-start.28 = (bf16[256,1024]{1,0:T(8,128)(2,1)}, bf16[256,1024]{1,0:T(8,128)(2,1)S(1)}, u32[]{:S(2)}, u32[]{:S(2)}) collective-permute-start(bf16[256,1024]{1,0:T(8,128)(2,1)} %copy-done.10), channel_id=1, source_target_pairs={{0,4},{4,0},{8,12},{12,8},{16,20},{20,16},{24,28},{28,24},{1,5},{5... | collective-permute-start | bytes 1572872 | tf_op jit(solution)/shard_map/ppermute | solution.py:39
  160.2 24.4 %collective-permute-start.29 = (bf16[256,1024]{1,0:T(8,128)(2,1)}, bf16[256,1024]{1,0:T(8,128)(2,1)S(1)}, u32[]{:S(2)}, u32[]{:S(2)}) collective-permute-start(bf16[256,1024]{1,0:T(8,128)(2,1)} %collective-permute-done.27.refs_5_), channel_id=1, source_target_pairs={{0,4},{4,0},{8,12},{12,8},{16,20},{20,16},{24,28},{28,24},{1,5},{5... | collective-permute-start | bytes 1572872 | tf_op jit(solution)/shard_map/ppermute | solution.py:39
  160.3 24.4 %collective-permute-start.33 = (bf16[1,256,512]{2,1,0:T(8,128)(2,1)}, bf16[1,256,512]{2,1,0:T(8,128)(2,1)S(1)}, u32[]{:S(2)}, u32[]{:S(2)}) collective-permute-start(bf16[1,256,512]{2,1,0:T(8,128)(2,1)} %collective-permute-done.31.refs_9_), channel_id=1, source_target_pairs={{0,4},{4,0},{8,12},{12,8},{16,20},{20,16},{24,28},{28,24},{1,5},{5... | collective-permute-start | bytes 786440 | tf_op jit(solution)/shard_map/ppermute | solution.py:39
  160.7 23.9 %collective-permute-start.32 = (bf16[1,256,512]{2,1,0:T(8,128)(2,1)}, bf16[1,256,512]{2,1,0:T(8,128)(2,1)S(1)}, u32[]{:S(2)}, u32[]{:S(2)}) collective-permute-start(bf16[1,256,512]{2,1,0:T(8,128)(2,1)} %collective-permute-done.30.refs_8_), channel_id=1, source_target_pairs={{0,4},{4,0},{8,12},{12,8},{16,20},{20,16},{24,28},{28,24},{1,5},{5... | collective-permute-start | bytes 786440 | tf_op jit(solution)/shard_map/ppermute | solution.py:39
  196.2 9.8 %collective-permute-start.44 = (bf16[64,1536]{1,0:T(8,128)(2,1)S(1)}, bf16[64,1536]{1,0:T(8,128)(2,1)S(1)}, u32[]{:S(2)}, u32[]{:S(2)}) collective-permute-start(bf16[64,1536]{1,0:T(8,128)(2,1)S(1)} %get-tuple-element.37), channel_id=1, source_target_pairs={{0,1},{1,2},{2,3},{3,0},{4,5},{5,6},{6,7},{7,4},{8,9},{9,10},{10,1... | collective-permute-start | bytes 589832 | tf_op jit(solution)/shard_map/ppermute | solution.py:44
  197.2 17.2 %collective-permute-start.45 = (bf16[64,1536]{1,0:T(8,128)(2,1)S(1)}, bf16[64,1536]{1,0:T(8,128)(2,1)S(1)}, u32[]{:S(2)}, u32[]{:S(2)}) collective-permute-start(bf16[64,1536]{1,0:T(8,128)(2,1)S(1)} %get-tuple-element.38), channel_id=1, source_target_pairs={{0,2},{1,3},{2,0},{3,1},{4,6},{5,7},{6,4},{7,5},{8,10},{9,11},{10,... | collective-permute-start | bytes 589832 | tf_op jit(solution)/shard_map/ppermute | solution.py:44
  199.0 15.5 %collective-permute-start.46 = (bf16[64,1536]{1,0:T(8,128)(2,1)S(1)}, bf16[64,1536]{1,0:T(8,128)(2,1)S(1)}, u32[]{:S(2)}, u32[]{:S(2)}) collective-permute-start(bf16[64,1536]{1,0:T(8,128)(2,1)S(1)} %get-tuple-element.39), channel_id=1, source_target_pairs={{0,3},{1,0},{2,1},{3,2},{4,7},{5,4},{6,5},{7,6},{8,11},{9,8},{10,9... | collective-permute-start | bytes 589832 | tf_op jit(solution)/shard_map/ppermute | solution.py:44
  200.1 29.7 %collective-permute-start.38 = (bf16[64,1536]{1,0:T(8,128)(2,1)S(1)}, bf16[64,1536]{1,0:T(8,128)(2,1)S(1)}, u32[]{:S(2)}, u32[]{:S(2)}) collective-permute-start(bf16[64,1536]{1,0:T(8,128)(2,1)S(1)} %get-tuple-element.28), channel_id=1, source_target_pairs={{0,1},{1,2},{2,3},{3,0},{4,5},{5,6},{6,7},{7,4},{8,9},{9,10},{10,1... | collective-permute-start | bytes 589832 | tf_op jit(solution)/shard_map/ppermute | solution.py:44
  201.0 31.9 %collective-permute-start.39 = (bf16[64,1536]{1,0:T(8,128)(2,1)S(1)}, bf16[64,1536]{1,0:T(8,128)(2,1)S(1)}, u32[]{:S(2)}, u32[]{:S(2)}) collective-permute-start(bf16[64,1536]{1,0:T(8,128)(2,1)S(1)} %get-tuple-element.29), channel_id=1, source_target_pairs={{0,2},{1,3},{2,0},{3,1},{4,6},{5,7},{6,4},{7,5},{8,10},{9,11},{10,... | collective-permute-start | bytes 589832 | tf_op jit(solution)/shard_map/ppermute | solution.py:44
  206.0 26.9 %collective-permute-start.40 = (bf16[64,1536]{1,0:T(8,128)(2,1)S(1)}, bf16[64,1536]{1,0:T(8,128)(2,1)S(1)}, u32[]{:S(2)}, u32[]{:S(2)}) collective-permute-start(bf16[64,1536]{1,0:T(8,128)(2,1)S(1)} %get-tuple-element.30), channel_id=1, source_target_pairs={{0,3},{1,0},{2,1},{3,2},{4,7},{5,4},{6,5},{7,6},{8,11},{9,8},{10,9... | collective-permute-start | bytes 589832 | tf_op jit(solution)/shard_map/ppermute | solution.py:44
  216.6 24.0 %collective-permute-start.47 = (bf16[64,512]{1,0:T(8,128)(2,1)S(1)}, bf16[64,512]{1,0:T(8,128)(2,1)S(1)}, u32[]{:S(2)}, u32[]{:S(2)}) collective-permute-start(bf16[64,512]{1,0:T(8,128)(2,1)S(1)} %get-tuple-element.41), channel_id=1, source_target_pairs={{0,1},{1,2},{2,3},{3,0},{4,5},{5,6},{6,7},{7,4},{8,9},{9,10},{10,1... | collective-permute-start | bytes 196616 | tf_op jit(solution)/shard_map/ppermute | solution.py:44
  229.8 13.2 %collective-permute-start.48 = (bf16[64,512]{1,0:T(8,128)(2,1)S(1)}, bf16[64,512]{1,0:T(8,128)(2,1)S(1)}, u32[]{:S(2)}, u32[]{:S(2)}) collective-permute-start(bf16[64,512]{1,0:T(8,128)(2,1)S(1)} %get-tuple-element.42), channel_id=1, source_target_pairs={{0,2},{1,3},{2,0},{3,1},{4,6},{5,7},{6,4},{7,5},{8,10},{9,11},{10,... | collective-permute-start | bytes 196616 | tf_op jit(solution)/shard_map/ppermute | solution.py:44
  229.8 13.2 %collective-permute-start.49 = (bf16[64,512]{1,0:T(8,128)(2,1)S(1)}, bf16[64,512]{1,0:T(8,128)(2,1)S(1)}, u32[]{:S(2)}, u32[]{:S(2)}) collective-permute-start(bf16[64,512]{1,0:T(8,128)(2,1)S(1)} %get-tuple-element.43), channel_id=1, source_target_pairs={{0,3},{1,0},{2,1},{3,2},{4,7},{5,4},{6,5},{7,6},{8,11},{9,8},{10,9... | collective-permute-start | bytes 196616 | tf_op jit(solution)/shard_map/ppermute | solution.py:44
  (48 other events, 556.9 us)
